TPU v7x, 32 devices: a whole 2x2x4 slice. The times are simulated.
32 devices in a mesh: replica: 8 (over z, core), fsdp: 4 (over y, x).
Axes of the slice: x: 2, y: 2, z: 4, core: 2. Of those that a mesh axis runs over, the one named last changes fastest.
Arguments:
- tokens: bfloat16 [2, 2048, 2048], P(None, ('replica', 'fsdp')), may hold values from -6 to 6
- cotangent: bfloat16 [2, 2048, 2048], P(None, ('replica', 'fsdp'))
- parents: int32 [2, 8, 13], P(None, 'replica'), may hold values from 0 to 11, as said below
- lengths: int32 [2, 8, 13], P(None, 'replica'), may hold values from 1 to 128, 256 in all within a row
- qkv_weight: bfloat16 [3, 2048, 2048], P(None, None, 'fsdp')
- out_weight: bfloat16 [2048, 2048], P('fsdp'), may hold values from -0.125 to 0.125
- gate_up_weight: bfloat16 [2, 2048, 8192], P(None, None, 'fsdp'), may hold values from -0.125 to 0.125
- down_weight: bfloat16 [8192, 2048], P('fsdp'), may hold values from -0.0625 to 0.0625
- qk_gain: float32 [2, 2048], P(None, 'fsdp'), may hold values from 1.1 to 1.9
- post_gain: float32 [2, 2048], replicated, may hold values from 0.5 to 1.5
Outputs:
- output: float32 [2, 2048, 2048], P(None, ('replica', 'fsdp'))
- input_grad: float32 [2, 2048, 2048], P(None, ('replica', 'fsdp'))
- qkv_grad: float32 [3, 2048, 2048], P(None, 'replica', 'fsdp')
- out_grad: float32 [2048, 2048], P('fsdp', 'replica')
- gate_up_grad: float32 [2, 2048, 8192], P(None, 'replica', 'fsdp')
- down_grad: float32 [8192, 2048], P('fsdp', 'replica')
- qk_gain_grad: float32 [2, 2048], P(None, 'fsdp')
- post_gain_grad: float32 [2, 2048], P(None, 'fsdp')
Inputs may be any that keep to these rules, and one draw needn't show every extreme that they name: parents[..., 0] = 0 and parents[..., s] < s for every later segment s, so a tree's root is segment 0. The lengths of one tree add up to 256, and the largest is exactly 128.
All inputs are finite; a program needn't handle non-finite values.
Results may differ from a plain program's by a relative error of at most 0.02.
Values may be sent and summed in bfloat16 or wider, within the bound.
No kernel may reach another device: no remote copies, remote signals or barrier semaphores. Data moves between devices by JAX's collectives and lax.ppermute only.
A program may use at most 256 MiB of HBM per device.

v0:
```python
import jax
import jax.numpy as jnp
from jax import lax
from jax.experimental import pallas as pl
from jax.experimental.pallas import tpu as pltpu
from jax.sharding import PartitionSpec as P

HD = 128


EPSILON = 1e-06
ROPE_BASE = 500000.0
BF = jnp.bfloat16
F32 = jnp.float32


def exchange(value, axis, flip):
    size = lax.axis_size(axis)
    return lax.ppermute(value, axis, [(i, i ^ flip) for i in range(size)])


def gather_blocks(rows):
    return [rows] + [exchange(rows, "fsdp", flip) for flip in range(1, lax.axis_size("fsdp"))]


def swap_blocks(blocks):
    return [blocks[0]] + [exchange(blocks[flip], "fsdp", flip) for flip in range(1, len(blocks))]


def cost(flops, moved, transcendentals=0):
    return (flops, moved, transcendentals)


class Order(list):
    pace = 0.001


def shape(dims, kind):
    return jax.ShapeDtypeStruct(dims, kind)


def dot(left, right):
    return jnp.dot(left, right, preferred_element_type=F32)


def dot_t(left, right):
    return lax.dot_general(left, right, (((1,), (1,)), ((), ())), preferred_element_type=F32)


def t_dot(left, right):
    return lax.dot_general(left, right, (((0,), (0,)), ((), ())), preferred_element_type=F32)


def lane_sums(field):
    ones = jnp.ones((8, field.shape[1]), F32)
    return lax.dot_general(
        ones,
        field,
        (((1,), (1,)), ((), ())),
        precision=lax.Precision.HIGHEST,
        preferred_element_type=F32,
    )


def join(block_refs, rows_ref):
    tok = block_refs[0].shape[0]
    for j, block_ref in enumerate(block_refs):
        rows_ref[pl.ds(j * tok, tok), :] = block_ref[...]


def write_blocks(rows, block_refs):
    tok = block_refs[0].shape[0]
    for j, block_ref in enumerate(block_refs):
        block_ref[...] = rows[j * tok : (j + 1) * tok].astype(block_ref.dtype)


def block_shapes(count, tok, width):
    return [shape((tok, width), F32)] + [shape((tok, width), BF)] * (count - 1)


def aligned_total(parts, tok):
    total = parts[0].T
    count = len(parts)
    for flip in range(1, count):
        column = parts[flip].T
        total = total + jnp.concatenate(
            [column[(j ^ flip) * tok : ((j ^ flip) + 1) * tok] for j in range(count)], axis=0
        )
    return total


def turn(field, cos_t, sin_t):
    return field * cos_t + pltpu.roll(field, HD // 2, 1) * sin_t


def turn_back(field, cos_t, sin_t):
    return field * cos_t - pltpu.roll(field, HD // 2, 1) * sin_t


VMEM = pl.BlockSpec(memory_space=pltpu.VMEM)
WHOLE = pltpu.CompilerParams(dimension_semantics=("arbitrary",))


def launch(
    order, kernel, args, in_specs, grid_spec=None, *, cost_estimate, pace=None, **settings
):
    waits = list(order)
    count = len(args)

    def body(*refs):
        kernel(*refs[:count], *refs[count + len(waits) :])

    flops, moved, transcendentals = [
        int(part * (order.pace if pace is None else pace)) for part in cost_estimate
    ]
    settings["cost_estimate"] = pl.CostEstimate(
        flops=flops, bytes_accessed=moved, transcendentals=transcendentals
    )
    specs = list(in_specs) + [pl.BlockSpec(memory_space=pl.ANY)] * len(waits)
    if grid_spec is None:
        settings["in_specs"] = specs
    else:
        settings["grid_spec"] = grid_spec(specs)
    settings["name"] = kernel.__qualname__.split(".<")[0].replace(".", "_")
    results = pl.pallas_call(body, **settings)(*args, *waits)
    order[:] = [results[0] if isinstance(results, (list, tuple)) else results]
    return results


def fence(order, arrays):
    order.extend(arrays)

    def kernel(out_ref):
        out_ref[...] = jnp.zeros((8, HD), F32)

    launch(
        order,
        kernel,
        [],
        in_specs=[],
        out_shape=shape((8, HD), F32),
        out_specs=VMEM,
        cost_estimate=cost(1 << 40, 1 << 30),
        pace=1,
    )


def gate(order, arrays):
    def kernel(*refs):
        pass

    held = pl.BlockSpec(memory_space=pl.ANY)
    return launch(
        order,
        kernel,
        arrays,
        in_specs=[held] * len(arrays),
        out_shape=[shape(array.shape, array.dtype) for array in arrays],
        out_specs=[held] * len(arrays),
        input_output_aliases={k: k for k in range(len(arrays))},
        cost_estimate=cost(0, 1000),
    )


def project(order, x_blocks, qkv_weight):
    count = len(x_blocks)
    tok, model_width = x_blocks[0].shape
    rows = count * tok
    width = qkv_weight.shape[2]

    def kernel(*refs):
        x_refs = refs[:count]
        weight_ref, raw_ref, values_ref, squares_ref, x_ref = refs[count:]
        step = pl.program_id(0)

        @pl.when(step == 0)
        def _():
            join(x_refs, x_ref)

        product = dot(x_ref[...], weight_ref[...])

        @pl.when(step < 2)
        def _():
            raw_ref[...] = product
            squares_ref[pl.ds(step, 1), :] = lane_sums(product * product)[:1]

        @pl.when(step == 2)
        def _():
            values_ref[...] = product.astype(BF)
            squares_ref[2:, :] = jnp.zeros((6, rows), F32)

    whole = pl.BlockSpec((tok, model_width), lambda n: (0, 0))
    return launch(
        order,
        kernel,
        [*x_blocks, qkv_weight],
        out_shape=[
            shape((2, rows, width), F32),
            shape((rows, width), BF),
            shape((8, rows), F32),
            shape((rows, model_width), BF),
        ],
        grid=(3,),
        in_specs=[whole] * count + [pl.BlockSpec((None, model_width, width), lambda n: (n, 0, 0))],
        out_specs=[
            pl.BlockSpec((None, rows, width), lambda n: (jnp.minimum(n, 1), 0, 0)),
            pl.BlockSpec((rows, width), lambda n: (0, 0)),
            pl.BlockSpec((8, rows), lambda n: (0, 0)),
            pl.BlockSpec((rows, model_width), lambda n: (0, 0)),
        ],
        compiler_params=WHOLE,
        cost_estimate=cost(6 * rows * model_width * width, 6 * model_width * width + 8 * rows * width),
    )


def pick(ref, m, each, tok, at):
    return jnp.concatenate(
        [
            ref[pl.ds(pl.multiple_of(j * tok + m * each, each), each), at]
            for j in range(ref.shape[0] // tok)
        ],
        axis=0,
    )


def place(ref, m, each, tok, at, rows):
    for j in range(ref.shape[0] // tok):
        ref[pl.ds(pl.multiple_of(j * tok + m * each, each), each), at] = rows[
            j * each : (j + 1) * each
        ]


def attend(order, raw, values, squares, tables, qk_gain, out_weight):
    count = len(squares)
    micro = tables[0].shape[0]
    _, rows, width = raw.shape
    heads = width // HD
    tok = rows // count
    each = tok // micro
    pack = rows // micro
    model_width = out_weight.shape[1]
    total_width = model_width
    scale = HD ** (-0.5)

    def kernel(
        raw_ref, values_ref, gain_ref, out_weight_ref, bias_ref, cos_ref, sin_ref, *refs
    ):
        parts = [ref[...] for ref in refs[:count]]
        context_ref, queries_ref, keys_ref, inv_ref = refs[count : count + 4]
        block_refs = refs[count + 4 :]
        inv_ref[...] = lax.rsqrt(aligned_total(parts, tok) / total_width + EPSILON)

        def one(m, carry):
            bias_v, cos_v, sin_v = bias_ref[m], cos_ref[m], sin_ref[m]
            inv = pick(inv_ref, m, each, tok, slice(None))
            own = pl.ds(pl.multiple_of(m * pack, pack), pack)
            for h in range(heads):
                at = slice(h * HD, (h + 1) * HD)
                q_raw = pick(raw_ref.at[0], m, each, tok, at)
                k_raw = pick(raw_ref.at[1], m, each, tok, at)
                q = turn(q_raw * inv[:, 0:1] * gain_ref[0:1, at], cos_v, sin_v).astype(BF)
                k = turn(k_raw * inv[:, 1:2] * gain_ref[1:2, at], cos_v, sin_v).astype(BF)
                queries_ref[own, at] = q
                keys_ref[own, at] = k
                scores = dot_t(q, k) * scale + bias_v
                weights = jnp.exp(scores - jnp.max(scores, axis=1, keepdims=True))
                probs = (weights / jnp.sum(weights, axis=1, keepdims=True)).astype(BF)
                context = dot(probs, pick(values_ref, m, each, tok, at)).astype(BF)
                place(context_ref, m, each, tok, at, context)
            return carry

        lax.fori_loop(0, micro, one, 0)
        write_blocks(dot(context_ref[...], out_weight_ref[...]), block_refs)

    return launch(
        order,
        kernel,
        [raw, values, qk_gain, out_weight, *tables, *squares],
        out_shape=[
            shape((rows, width), BF),
            shape((rows, width), BF),
            shape((rows, width), BF),
            shape((rows, 8), F32),
        ]
        + block_shapes(count, tok, model_width),
        in_specs=[VMEM] * (7 + count),
        out_specs=[VMEM] * (4 + count),
        cost_estimate=cost(
            4 * rows * pack * width + 2 * rows * width * model_width,
            2 * width * model_width + 14 * rows * width + 2 * rows * model_width,
            heads * rows * pack,
        ),
    )


def attend_back(order, d_attn_blocks, out_weight, queries, keys, values, raw, inv, tables, qk_gain):
    count = len(d_attn_blocks)
    micro = tables[0].shape[0]
    tok, model_width = d_attn_blocks[0].shape
    _, rows, width = raw.shape
    heads = width // HD
    each = tok // micro
    pack = rows // micro
    scale = HD ** (-0.5)

    def kernel(*refs):
        block_refs = refs[:count]
        (
            bias_ref,
            cos_ref,
            sin_ref,
            out_weight_ref,
            queries_ref,
            keys_ref,
            values_ref,
            raw_ref,
            inv_ref,
            gain_ref,
            d_attn_ref,
            d_norm_ref,
            d_values_ref,
            sums_ref,
            gain_sums_ref,
            d_context_ref,
            totals_ref,
        ) = refs[count:]
        join(block_refs, d_attn_ref)
        d_context_ref[...] = dot_t(d_attn_ref[...], out_weight_ref[...]).astype(BF)
        gain_sums_ref[...] = jnp.zeros((2, width), F32)

        def one(m, carry):
            bias_v, cos_v, sin_v = bias_ref[m], cos_ref[m], sin_ref[m]
            inv = pick(inv_ref, m, each, tok, slice(None))
            own = pl.ds(pl.multiple_of(m * pack, pack), pack)
            totals = [jnp.zeros((pack, HD), F32), jnp.zeros((pack, HD), F32)]
            for h in range(heads):
                at = slice(h * HD, (h + 1) * HD)
                q, k = queries_ref[own, at], keys_ref[own, at]
                v = pick(values_ref, m, each, tok, at)
                d_out = pick(d_context_ref, m, each, tok, at)
                scores = dot_t(q, k) * scale + bias_v
                weights = jnp.exp(scores - jnp.max(scores, axis=1, keepdims=True))
                probs = weights / jnp.sum(weights, axis=1, keepdims=True)
                d_probs = dot_t(d_out, v)
                delta = jnp.sum(d_probs * probs, axis=1, keepdims=True)
                d_scores = (probs * (d_probs - delta)).astype(BF)
                d_values = t_dot(probs.astype(BF), d_out).astype(BF)
                place(d_values_ref, m, each, tok, at, d_values)
                turned = (dot(d_scores, k) * scale, t_dot(d_scores, q) * scale)
                for n in range(2):
                    d_norm = turn_back(turned[n], cos_v, sin_v)
                    place(d_norm_ref.at[n], m, each, tok, at, d_norm)
                    field = pick(raw_ref.at[n], m, each, tok, at) * d_norm
                    totals[n] += field * gain_ref[n : n + 1, at]
                    gain_sums_ref[n : n + 1, at] += jnp.sum(
                        field * inv[:, n : n + 1], axis=0, keepdims=True
                    )
            for n in range(2):
                place(totals_ref.at[n], m, each, tok, slice(None), totals[n])
            return carry

        lax.fori_loop(0, micro, one, 0)
        for n in range(2):
            sums_ref[n : n + 1, :] = lane_sums(totals_ref[n])[:1]
        sums_ref[2:, :] = jnp.zeros((6, rows), F32)

    return launch(
        order,
        kernel,
        [*d_attn_blocks, *tables, out_weight, queries, keys, values, raw, inv, qk_gain],
        out_shape=[
            shape((rows, model_width), BF),
            shape((2, rows, width), F32),
            shape((rows, width), BF),
            shape((8, rows), F32),
            shape((2, width), F32),
        ],
        in_specs=[VMEM] * (10 + count),
        out_specs=[VMEM] * 5,
        scratch_shapes=[pltpu.VMEM((rows, width), BF), pltpu.VMEM((2, rows, HD), F32)],
        cost_estimate=cost(
            10 * rows * pack * width + 2 * rows * width * model_width,
            2 * width * model_width + 24 * rows * width + 2 * rows * model_width,
            heads * rows * pack,
        ),
    )


def project_back(order, d_norm, d_values, raw, inv, sums, qk_gain, qkv_weight):
    count = len(sums)
    _, rows, width = raw.shape
    tok = rows // count
    model_width = qkv_weight.shape[1]

    def kernel(d_norm_ref, d_values_ref, raw_ref, inv_ref, gain_ref, weight_ref, *refs):
        parts = refs[:count]
        d_projected_ref = refs[count]
        block_refs = refs[count + 1 : 2 * count + 1]
        total_ref = refs[2 * count + 1]
        step = pl.program_id(0)
        inv = inv_ref[...]

        @pl.when(step == 0)
        def _():
            d_projected_ref[...] = d_values_ref[...]

        @pl.when(step > 0)
        def _():
            shared = aligned_total([part[...] for part in parts], tok)
            first = step == 1
            r = jnp.where(first, inv[:, 0:1], inv[:, 1:2])
            s = jnp.where(first, shared[:, 0:1], shared[:, 1:2])
            gain = jnp.where(first, gain_ref[0:1, :], gain_ref[1:2, :])
            d_projected_ref[...] = (
                r * (d_norm_ref[...] * gain) - raw_ref[...] * (r * r * r * s / model_width)
            ).astype(BF)

        product = dot_t(d_projected_ref[...], weight_ref[...])

        total_ref[...] = jnp.where(step == 0, 0.0, total_ref[...]) + product

        @pl.when(step == 2)
        def _():
            write_blocks(total_ref[...], block_refs)

    def part_at(n):
        return lax.rem(n + 2, 3)

    field = pl.BlockSpec((None, rows, width), lambda n: (jnp.maximum(n - 1, 0), 0, 0))
    return launch(
        order,
        kernel,
        [d_norm, d_values, raw, inv, qk_gain, qkv_weight, *sums],
        out_shape=[shape((3, rows, width), BF)] + block_shapes(count, tok, model_width),
        grid=(3,),
        in_specs=[
            field,
            pl.BlockSpec((rows, width), lambda n: (0, 0)),
            field,
            pl.BlockSpec((rows, 8), lambda n: (0, 0)),
            pl.BlockSpec((2, width), lambda n: (0, 0)),
            pl.BlockSpec((None, model_width, width), lambda n: (part_at(n), 0, 0)),
        ]
        + [pl.BlockSpec((8, rows), lambda n: (0, 0))] * count,
        out_specs=[pl.BlockSpec((None, rows, width), lambda n: (part_at(n), 0, 0))]
        + [pl.BlockSpec((tok, model_width), lambda n: (0, 0))] * count,
        scratch_shapes=[pltpu.VMEM((rows, model_width), F32)],
        compiler_params=WHOLE,
        cost_estimate=cost(
            6 * rows * model_width * width, 6 * model_width * width + 22 * rows * width + 2 * rows * model_width
        ),
    )


def mlp_forward(order, hidden_blocks, gate_up_weight, down_weight):
    count = len(hidden_blocks)
    tok, model_width = hidden_blocks[0].shape
    rows = count * tok
    units = down_weight.shape[0]
    tile = min(512, units)
    last = units // tile - 1

    def kernel(*refs):
        gate_w_ref, up_w_ref, down_w_ref, gate_up_ref, swiglu_ref, hidden_ref = refs[
            count : count + 6
        ]
        block_refs = refs[count + 6 : 2 * count + 6]
        total_ref = refs[2 * count + 6]
        step = pl.program_id(0)

        @pl.when(step == 0)
        def _():
            join(refs[:count], hidden_ref)

        gate = dot(hidden_ref[...], gate_w_ref[...])
        up = dot(hidden_ref[...], up_w_ref[...])
        swiglu = (gate * jax.nn.sigmoid(gate) * up).astype(BF)
        gate_up_ref[0] = gate.astype(BF)
        gate_up_ref[1] = up.astype(BF)
        swiglu_ref[...] = swiglu
        product = dot(swiglu, down_w_ref[...])

        total_ref[...] = jnp.where(step == 0, 0.0, total_ref[...]) + product

        @pl.when(step == last)
        def _():
            write_blocks(total_ref[...], block_refs)

    field = pl.BlockSpec((rows, tile), lambda f: (0, f))
    return launch(
        order,
        kernel,
        [*hidden_blocks, gate_up_weight, gate_up_weight, down_weight],
        out_shape=[
            shape((2, rows, units), BF),
            shape((rows, units), BF),
            shape((rows, model_width), BF),
        ]
        + block_shapes(count, tok, model_width),
        grid=(units // tile,),
        in_specs=[pl.BlockSpec((tok, model_width), lambda f: (0, 0))] * count
        + [
            pl.BlockSpec((None, model_width, tile), lambda f: (0, 0, f)),
            pl.BlockSpec((None, model_width, tile), lambda f: (1, 0, f)),
            pl.BlockSpec((tile, model_width), lambda f: (f, 0)),
        ],
        out_specs=[pl.BlockSpec((2, rows, tile), lambda f: (0, 0, f)), field]
        + [pl.BlockSpec((rows, model_width), lambda f: (0, 0))]
        + [pl.BlockSpec((tok, model_width), lambda f: (0, 0))] * count,
        scratch_shapes=[pltpu.VMEM((rows, model_width), F32)],
        compiler_params=WHOLE,
        cost_estimate=cost(
            6 * rows * model_width * units,
            6 * model_width * units + 6 * rows * units + 8 * rows * model_width,
            rows * units,
        ),
    )


def unit_grads(gate, up, d_swiglu):
    sigmoid = jax.nn.sigmoid(gate)
    d_gate = d_swiglu * up * sigmoid * (1.0 + gate * (1.0 - sigmoid))
    return (d_gate.astype(BF), (d_swiglu * (gate * sigmoid)).astype(BF))


def mlp_back(order, d_mlp_blocks, gate_up, gate_up_weight, down_weight):
    count = len(d_mlp_blocks)
    tok, model_width = d_mlp_blocks[0].shape
    rows = count * tok
    units = down_weight.shape[0]
    tile = min(512, units)
    last = units // tile - 1

    def kernel(*refs):
        gate_up_ref, gate_w_ref, up_w_ref, down_w_ref, d_gate_up_ref, d_mlp_ref = refs[
            count : count + 6
        ]
        block_refs = refs[count + 6 : 2 * count + 6]
        total_ref = refs[2 * count + 6]
        step = pl.program_id(0)

        @pl.when(step == 0)
        def _():
            join(refs[:count], d_mlp_ref)

        d_swiglu = dot_t(d_mlp_ref[...], down_w_ref[...])
        d_gate, d_up = unit_grads(gate_up_ref[0].astype(F32), gate_up_ref[1].astype(F32), d_swiglu)
        d_gate_up_ref[0] = d_gate
        d_gate_up_ref[1] = d_up
        product = dot_t(d_gate, gate_w_ref[...]) + dot_t(d_up, up_w_ref[...])

        total_ref[...] = jnp.where(step == 0, 0.0, total_ref[...]) + product

        @pl.when(step == last)
        def _():
            write_blocks(total_ref[...], block_refs)

    field = pl.BlockSpec((2, rows, tile), lambda f: (0, 0, f))
    return launch(
        order,
        kernel,
        [*d_mlp_blocks, gate_up, gate_up_weight, gate_up_weight, down_weight],
        out_shape=[shape((2, rows, units), BF), shape((rows, model_width), BF)]
        + block_shapes(count, tok, model_width),
        grid=(units // tile,),
        in_specs=[pl.BlockSpec((tok, model_width), lambda f: (0, 0))] * count
        + [
            field,
            pl.BlockSpec((None, model_width, tile), lambda f: (0, 0, f)),
            pl.BlockSpec((None, model_width, tile), lambda f: (1, 0, f)),
            pl.BlockSpec((tile, model_width), lambda f: (f, 0)),
        ],
        out_specs=[field]
        + [pl.BlockSpec((rows, model_width), lambda f: (0, 0))]
        + [pl.BlockSpec((tok, model_width), lambda f: (0, 0))] * count,
        scratch_shapes=[pltpu.VMEM((rows, model_width), F32)],
        compiler_params=WHOLE,
        cost_estimate=cost(
            6 * rows * model_width * units,
            6 * model_width * units + 8 * rows * units + 8 * rows * model_width,
            rows * units,
        ),
    )


def mlp_units(order, hidden_blocks, d_mlp_blocks, gate_up_weight, down_weight):
    count = len(d_mlp_blocks)
    tok, model_width = d_mlp_blocks[0].shape
    rows = count * tok
    units = down_weight.shape[0]
    tile = min(256, units)

    def kernel(*refs):
        gate_w_ref, up_w_ref, down_w_ref = refs[2 * count : 2 * count + 3]
        d_gate_up_ref, swiglu_ref, d_mlp_ref, hidden_ref = refs[2 * count + 3 :]

        @pl.when(pl.program_id(0) == 0)
        def _():
            join(refs[:count], hidden_ref)
            join(refs[count : 2 * count], d_mlp_ref)

        gate = dot(hidden_ref[...], gate_w_ref[...])
        up = dot(hidden_ref[...], up_w_ref[...])
        d_gate, d_up = unit_grads(gate, up, dot_t(d_mlp_ref[...], down_w_ref[...]))
        swiglu_ref[...] = (gate * jax.nn.sigmoid(gate) * up).astype(BF)
        d_gate_up_ref[0] = d_gate
        d_gate_up_ref[1] = d_up

    return launch(
        order,
        kernel,
        [*hidden_blocks, *d_mlp_blocks, gate_up_weight, gate_up_weight, down_weight],
        out_shape=[
            shape((2, rows, units), BF),
            shape((rows, units), BF),
            shape((rows, model_width), BF),
            shape((rows, model_width), BF),
        ],
        grid=(units // tile,),
        in_specs=[pl.BlockSpec((tok, model_width), lambda f: (0, 0))] * (2 * count)
        + [
            pl.BlockSpec((None, model_width, tile), lambda f: (0, 0, f)),
            pl.BlockSpec((None, model_width, tile), lambda f: (1, 0, f)),
            pl.BlockSpec((tile, model_width), lambda f: (f, 0)),
        ],
        out_specs=[
            pl.BlockSpec((2, rows, tile), lambda f: (0, 0, f)),
            pl.BlockSpec((rows, tile), lambda f: (0, f)),
            pl.BlockSpec((rows, model_width), lambda f: (0, 0)),
            pl.BlockSpec((rows, model_width), lambda f: (0, 0)),
        ],
        compiler_params=WHOLE,
        cost_estimate=cost(
            6 * rows * model_width * units,
            6 * rows * model_width + 6 * model_width * units + 6 * rows * units,
            rows * units,
        ),
    )


def sum_parts(part_refs):
    total = part_refs[0][...].astype(F32)
    for part_ref in part_refs[1:]:
        total += part_ref[...].astype(F32)
    return total


def norm_back(field, gain, upstream):
    width = field.shape[1]
    inv = lax.rsqrt(jnp.sum(field * field, axis=1, keepdims=True) / width + EPSILON)
    weighted = upstream * gain
    shared = jnp.sum(field * weighted, axis=1, keepdims=True)
    gain_sum = jnp.sum(upstream * field * inv, axis=0, keepdims=True)
    return (inv * weighted - field * (inv * inv * inv * shared / width), gain_sum)


def by_rows(order, kernel, parts, rows, gains, outs, sums, work):
    tok, width = rows[0].shape
    block = min(32, tok)
    cut = pl.BlockSpec((block, width), lambda i: (i, 0))
    return launch(
        order,
        kernel,
        [*parts, *rows, gains],
        in_specs=[cut] * (len(parts) + len(rows)) + [pl.BlockSpec(gains.shape, lambda i: (0, 0))],
        out_shape=[shape((tok, width), kind) for kind in outs] + [shape((1, width), F32)] * sums,
        grid=(tok // block,),
        out_specs=[cut] * len(outs) + [pl.BlockSpec((1, width), lambda i: (0, 0))] * sums,
        compiler_params=WHOLE,
        cost_estimate=cost(work * tok * width, 24 * tok * width),
    )


def add_rows(sum_ref, value):
    @pl.when(pl.program_id(0) == 0)
    def _():
        sum_ref[...] = value

    @pl.when(pl.program_id(0) > 0)
    def _():
        sum_ref[...] += value


def after_attention(order, parts, x_rows, post_gain):
    count = len(parts)

    def kernel(*refs):
        x_ref, gain_ref, attn_ref, hidden_ref, rounded_ref = refs[count:]
        attn = sum_parts(refs[:count])
        inv = lax.rsqrt(jnp.sum(attn * attn, axis=1, keepdims=True) / attn.shape[1] + EPSILON)
        hidden = x_ref[...].astype(F32) + attn * inv * gain_ref[0:1, :]
        attn_ref[...] = attn
        hidden_ref[...] = hidden
        rounded_ref[...] = hidden.astype(BF)

    return by_rows(order, kernel, parts, [x_rows], post_gain, [F32, F32, BF], 0, 8)


def after_mlp(order, parts, hidden, grad_rows, post_gain):
    count = len(parts)

    def kernel(*refs):
        hidden_ref, grad_ref, gain_ref, out_ref, d_mlp_ref, gain_sum_ref = refs[count:]
        mlp = sum_parts(refs[:count])
        gain = gain_ref[1:2, :]
        inv = lax.rsqrt(jnp.sum(mlp * mlp, axis=1, keepdims=True) / mlp.shape[1] + EPSILON)
        out_ref[...] = hidden_ref[...] + mlp * inv * gain
        d_mlp, gain_sum = norm_back(mlp, gain, grad_ref[...].astype(F32))
        d_mlp_ref[...] = d_mlp.astype(BF)
        add_rows(gain_sum_ref, gain_sum)

    return by_rows(order, kernel, parts, [hidden, grad_rows], post_gain, [F32, BF], 1, 16)


def before_attention(order, parts, grad_rows, attn, post_gain):
    count = len(parts)

    def kernel(*refs):
        grad_ref, attn_ref, gain_ref, d_hidden_ref, d_attn_ref, gain_sum_ref = refs[count:]
        d_hidden = grad_ref[...].astype(F32) + sum_parts(refs[:count])
        d_hidden_ref[...] = d_hidden
        d_attn, gain_sum = norm_back(attn_ref[...], gain_ref[0:1, :], d_hidden)
        d_attn_ref[...] = d_attn.astype(BF)
        add_rows(gain_sum_ref, gain_sum)

    return by_rows(order, kernel, parts, [grad_rows, attn], post_gain, [F32, BF], 1, 16)


def send_order(top):
    def halves(codes, bit):
        if len(codes) == 1:
            return codes
        return halves([c for c in codes if c & bit], 2 * bit) + halves(
            [c for c in codes if not c & bit], 2 * bit
        )

    stages = []
    bit = 1
    while bit < top:
        stages.append((bit, [bit + c for c in halves(list(range(0, top, 2 * bit)), 2 * bit)]))
        bit *= 2
    return stages


def grad_rows_of(order, splits, sets):
    codes = [code for split in splits for code in split]
    blocks = len(codes)
    replicas = lax.axis_size("replica")
    picks = lax.axis_index("replica") ^ jnp.array(codes, jnp.int32)
    block = sets[0][0].shape[1] // replicas
    planes, _, units = sets[0][1].shape
    tile = min(512, units)
    tiles = units // tile
    width = planes * units
    depth = sum(rows for _, _, _, rows in sets)
    count = len(sets)
    kinds = [BF] * (len(splits) - 1) + [F32]

    def kernel(picks_ref, *refs):
        left_refs = refs[: count * blocks]
        right_refs = refs[count * blocks : count * blocks + count]
        out_refs = refs[count * blocks + count : count * blocks + count + len(splits)]
        turned_ref, right_ref = refs[count * blocks + count + len(splits) :]

        @pl.when(pl.program_id(0) == 0)
        def _():
            at = 0
            for k, (_, _, _, rows) in enumerate(sets):
                for b in range(blocks):
                    turned_ref[pl.ds(b * block, block), pl.ds(at, rows)] = left_refs[k * blocks + b][
                        ...
                    ].T
                at += rows

        at = 0
        for k, (_, _, _, rows) in enumerate(sets):
            right_ref[pl.ds(at, rows), :] = right_refs[k][...]
            at += rows
        first = 0
        for split, out_ref in zip(splits, out_refs):
            rows = len(split) * block
            out_ref[...] = dot(turned_ref[pl.ds(first, rows), :], right_ref[...]).astype(out_ref.dtype)
            first += rows

    in_specs = [
        pl.BlockSpec((rows, block), lambda f, picks_ref, group=group, b=b: (group, picks_ref[b]))
        for _, _, group, rows in sets
        for b in range(blocks)
    ] + [
        pl.BlockSpec(
            (None, rows, tile),
            lambda f, picks_ref, group=group: (lax.div(f, tiles), group, lax.rem(f, tiles)),
        )
        for _, _, group, rows in sets
    ]
    return launch(
        order,
        kernel,
        [picks]
        + [left for left, _, _, _ in sets for _ in range(blocks)]
        + [right for _, right, _, _ in sets],
        in_specs,
        lambda specs: pltpu.PrefetchScalarGridSpec(
            num_scalar_prefetch=1,
            grid=(planes * tiles,),
            in_specs=specs,
            out_specs=[
                pl.BlockSpec((len(split) * block, tile), lambda f, picks_ref: (0, f))
                for split in splits
            ],
            scratch_shapes=[
                pltpu.VMEM((blocks * block, depth), BF),
                pltpu.VMEM((depth, tile), BF),
            ],
        ),
        out_shape=[shape((len(split) * block, width), kind) for split, kind in zip(splits, kinds)],
        compiler_params=WHOLE,
        cost_estimate=cost(
            2 * depth * blocks * block * width,
            2 * depth * (blocks * block + width) + 2 * blocks * block * width,
        ),
    )


def add_parts(order, own, adds, column, width):
    rows = own.shape[0]
    tile = min(2048, width)
    tiles = width // tile

    def kernel(own_ref, *refs):
        refs[-1][...] = sum_parts([own_ref, *refs[:-1]]).astype(BF)

    return launch(
        order,
        kernel,
        [own] + [array for array, _, _ in adds],
        in_specs=[
            pl.BlockSpec((rows, tile), lambda f, group=group, at=at: (group, at * tiles + f))
            for group, at in [(0, column)] + [(group, at) for _, group, at in adds]
        ],
        out_shape=shape((rows, width), BF),
        grid=(tiles,),
        out_specs=pl.BlockSpec((rows, tile), lambda f: (0, f)),
        compiler_params=WHOLE,
        cost_estimate=cost(rows * width * len(adds), 2 * rows * width * (2 + len(adds))),
    )


class OwnersSum:
    def __init__(self, order, sets, top, pieces=1):
        self.stages = send_order(top)
        self.outs = grad_rows_of(order, [codes for _, codes in self.stages] + [[0]], sets)
        self.pieces = pieces
        self.at = 0
        self.received = [[] for _ in range(pieces)]
        bit, codes = self.stages[0]
        whole = exchange(self.outs[0], "replica", bit)
        for n in range(pieces):
            self.received[n].append((whole, [code ^ bit for code in codes], n))

    def adds(self, n, codes):
        return [
            (array, held.index(codes[0]) // len(codes), column)
            for array, held, column in self.received[n]
        ]

    def latest(self, n=0):
        return self.received[n][-1][0]

    def step(self, order):
        self.at += 1
        for n in range(self.pieces):
            self.send(order, n)

    def send(self, order, n):
        bit, codes = self.stages[self.at]
        own = self.outs[self.at]
        sent = add_parts(order, own, self.adds(n, codes), n, own.shape[1] // self.pieces)
        self.received[n].append((exchange(sent, "replica", bit), [code ^ bit for code in codes], 0))

    def finish(self, order, planes, turned):
        kept = self.outs[-1]
        rows, width = kept.shape
        units = width // planes
        span = width // self.pieces
        tile = min(512 if turned else 1024, units)
        tiles = units // tile
        grid = planes * tiles
        count = grid // self.pieces
        adds = [
            (array, group, column * count if array.shape[1] == width else -1, n)
            for n in range(self.pieces)
            for array, group, column in self.adds(n, [0])
        ]
        each = len(adds) // self.pieces

        def kernel(kept_ref, *refs):
            out_ref = refs[-1]
            for n in range(self.pieces):

                @pl.when(lax.div(pl.program_id(0), count) == n)
                def _():
                    total = kept_ref[...]
                    for add_ref in refs[n * each : (n + 1) * each]:
                        total += add_ref[...].astype(F32)
                    out_ref[...] = total.T if turned else total

        def add_spec(group, whole, n):
            def at(f):
                own = jnp.clip(f - n * count, 0, count - 1)
                return (group, own + n * count if whole else own)

            return pl.BlockSpec((rows, tile), at)

        if turned:
            out_shape = shape((units, rows), F32)
            out_spec = pl.BlockSpec((tile, rows), lambda f: (f, 0))
        else:
            out_shape = shape((planes, rows, units), F32)
            out_spec = pl.BlockSpec(
                (None, rows, tile), lambda f: (lax.div(f, tiles), 0, lax.rem(f, tiles))
            )
        return launch(
            order,
            kernel,
            [kept] + [array for array, _, _, _ in adds],
            in_specs=[pl.BlockSpec((rows, tile), lambda f: (0, f))]
            + [add_spec(group, first >= 0, n) for _, group, first, n in adds],
            out_shape=out_shape,
            grid=(grid,),
            out_specs=out_spec,
            compiler_params=WHOLE,
            cost_estimate=cost(rows * width * len(adds), rows * width * (8 + 2 * each)),
        )


def true_rows(tok_dev):
    size = lax.axis_size("fsdp")
    block = jnp.arange(size, dtype=jnp.int32) ^ lax.axis_index("fsdp")
    return (block[:, None] * tok_dev + jnp.arange(tok_dev, dtype=jnp.int32)[None, :]).reshape(-1)


def tree_tables(parent_row, length_row, places):
    segments = parent_row.shape[0]
    labels = jnp.arange(segments, dtype=jnp.int32)
    before = labels[:, None] >= labels[None, :]
    ends = jnp.sum(jnp.where(before, length_row[None, :], 0), axis=1)
    starts = ends - length_row
    segment_of = jnp.sum((places[:, None] >= ends[None, :]).astype(jnp.int32), axis=1)
    member = segment_of[:, None] == labels[None, :]
    reach = ((labels[:, None] == labels[None, :]) | (parent_row[:, None] == labels[None, :])).astype(F32)
    steps = 1
    while steps < segments - 1:
        reach = (jnp.dot(reach, reach) > 0.5).astype(F32)
        steps *= 2
    ancestry = reach > 0.5
    above = jnp.sum(jnp.where(ancestry, length_row[None, :], 0), axis=1) - length_row
    moved = jnp.sum(jnp.where(member, (above - starts)[None, :], 0), axis=1)
    position = (places + moved).astype(F32)
    member_f = member.astype(F32)
    near = jnp.dot(jnp.dot(member_f, reach), member_f.T) > 0.5
    visible = near & (places[None, :] <= places[:, None])
    freq = ROPE_BASE ** (-jnp.arange(0, HD, 2, dtype=F32) / HD)
    angle = position[:, None] * freq[None, :]
    cos_half, sin_half = jnp.cos(angle), jnp.sin(angle)
    return (
        jnp.where(visible, 0.0, -1e30).astype(F32),
        jnp.concatenate([cos_half, cos_half], axis=1),
        jnp.concatenate([-sin_half, sin_half], axis=1),
    )


def on_device(
    tokens,
    cotangent,
    parents,
    lengths,
    qkv_weight,
    out_weight,
    gate_up_weight,
    down_weight,
    qk_gain,
    post_gain,
):
    micro, tok_dev, model_width = tokens.shape
    local_width = qkv_weight.shape[2]
    size = lax.axis_size("fsdp")
    replicas = lax.axis_size("replica")
    tok = micro * tok_dev
    rows = tok * size
    far = replicas // 2
    places = true_rows(tok_dev)
    x_rows = tokens.reshape(tok, model_width)
    grad_rows = cotangent.reshape(tok, model_width)
    order = Order()
    x_blocks = gather_blocks(x_rows)
    tables = jax.vmap(tree_tables, in_axes=(0, 0, None))(parents[:, 0], lengths[:, 0], places)
    raw, values, squares, x_full = project(order, x_blocks, qkv_weight)
    context, queries, keys, inv, *attn_blocks = attend(
        order, raw, values, gather_blocks(squares), tables, qk_gain, out_weight
    )
    attn, hidden, hidden_b = after_attention(order, swap_blocks(attn_blocks), x_rows, post_gain)
    hidden_blocks = gather_blocks(hidden_b)
    far_hidden_blocks = gather_blocks(exchange(hidden_b, "replica", far))
    gate_up, swiglu, hidden_full, *mlp_blocks = mlp_forward(
        order, hidden_blocks, gate_up_weight, down_weight
    )
    order.extend(far_hidden_blocks[1:])
    mlp_blocks = gate(order, mlp_blocks)
    out_rows, d_mlp, mlp_gain_sum = after_mlp(
        order, swap_blocks(mlp_blocks), hidden, grad_rows, post_gain
    )
    d_mlp_blocks = gather_blocks(d_mlp)
    far_d_mlp_blocks = gather_blocks(exchange(d_mlp, "replica", far))
    d_gate_up, d_mlp_full, *d_hidden_blocks = mlp_back(
        order, d_mlp_blocks, gate_up, gate_up_weight, down_weight
    )
    d_hidden_parts = swap_blocks(d_hidden_blocks)
    fence(order, far_d_mlp_blocks[1:])
    far_d_gate_up, far_swiglu, far_d_mlp, far_hidden = mlp_units(
        order, far_hidden_blocks, far_d_mlp_blocks, gate_up_weight, down_weight
    )
    gate_up_sum = OwnersSum(
        order, [(hidden_full, d_gate_up, 0, rows), (far_hidden, far_d_gate_up, 0, rows)], far, 2
    )
    d_hidden, d_attn, attn_gain_sum = before_attention(
        order, d_hidden_parts, grad_rows, attn, post_gain
    )
    d_attn_blocks = gather_blocks(d_attn)
    order.pace = 100
    down_sum = OwnersSum(
        order, [(d_mlp_full, swiglu[None], 0, rows), (far_d_mlp, far_swiglu[None], 0, rows)], far
    )
    order.pace = 0.001
    gate_up_sum.step(order)
    order.pace = 100
    d_attn_full, d_norm, d_values, sums, qk_gain_sums = attend_back(
        order, d_attn_blocks, out_weight, queries, keys, values, raw, inv, tables, qk_gain
    )
    order.pace = 0.001
    sums_parts = gather_blocks(sums)
    down_sum.step(order)
    order.append(gate_up_sum.latest(0))
    d_projected, *input_blocks = project_back(
        order, d_norm, d_values, raw, inv, sums_parts, qk_gain, qkv_weight
    )
    input_parts = swap_blocks(input_blocks)
    [gain_rows] = gate(order, [jnp.concatenate([attn_gain_sum, mlp_gain_sum], axis=0)])
    me = lax.axis_index("fsdp")
    split = gain_rows.reshape(2, size, local_width)
    post_rows = lax.dynamic_index_in_dim(split, me, 1, keepdims=False)
    for flip in range(1, size):
        sent = lax.dynamic_index_in_dim(split, me ^ flip, 1, keepdims=False)
        post_rows = post_rows + exchange(sent, "fsdp", flip)
    gains = jnp.concatenate([qk_gain_sums, post_rows], axis=0)
    gains = gains + exchange(gains, "replica", 1)
    order.append(gate_up_sum.latest(1))
    qkv_sum = OwnersSum(order, [(x_full, d_projected, 0, rows)], replicas, 3)
    out_sum = OwnersSum(order, [(d_attn_full, context[None], 0, rows)], replicas)
    fence(order, [down_sum.latest(), *input_parts[1:], gains])
    qkv_sum.step(order)
    out_sum.step(order)
    gate_up_grad = gate_up_sum.finish(order, 2, False)
    qkv_sum.at += 1
    qkv_sum.send(order, 0)
    down_grad = down_sum.finish(order, 1, True)
    qkv_sum.send(order, 1)
    order.append(qkv_sum.latest(0))
    qkv_sum.send(order, 2)
    order.append(qkv_sum.latest(1))
    out_sum.step(order)
    [gains] = gate(order, [gains])
    flip = 2
    while flip < far:
        gains = gains + exchange(gains, "replica", flip)
        flip *= 2
    order.append(gains)
    qkv_grad = qkv_sum.finish(order, 3, False)
    out_grad = out_sum.finish(order, 1, True)
    [far_gains] = gate(order, [exchange(gains, "replica", far)])
    gains = gains + far_gains
    input_grad = d_hidden + sum(part.astype(F32) for part in input_parts)
    return (
        out_rows.reshape(micro, tok_dev, model_width),
        input_grad.reshape(micro, tok_dev, model_width),
        qkv_grad,
        out_grad,
        gate_up_grad,
        down_grad,
        gains[:2],
        gains[2:],
    )


def solution(mesh):
    in_specs = (
        P(None, ("replica", "fsdp"), None),
        P(None, ("replica", "fsdp"), None),
        P(None, "replica", None),
        P(None, "replica", None),
        P(None, None, "fsdp"),
        P("fsdp", None),
        P(None, None, "fsdp"),
        P("fsdp", None),
        P(None, "fsdp"),
        P(),
    )
    out_specs = (
        P(None, ("replica", "fsdp"), None),
        P(None, ("replica", "fsdp"), None),
        P(None, "replica", "fsdp"),
        P("fsdp", "replica"),
        P(None, "replica", "fsdp"),
        P("fsdp", "replica"),
        P(None, "fsdp"),
        P(None, "fsdp"),
    )
    return jax.shard_map(
        on_device, mesh=mesh, in_specs=in_specs, out_specs=out_specs, check_vma=False
    )
```

profile of v0, /device:TPU:0, one launch (start us, length us, event | category | flops | bytes accessed | tf_op | source)
XLA Modules:
  0.0 444.0 jit_solution(3630488127242248096)
XLA Ops:
  10.9 5.7 %collective-permute-done.refs_1_ = bf16[128,2048]{1,0:T(8,128)(2,1)S(1)} collective-permute-done((bf16[128,2048]{1,0:T(8,128)(2,1)}, bf16[128,2048]{1,0:T(8,128)(2,1)S(1)}, u32[]{:S(2)}, u32[]{:S(2)}) %collective-permute-start) | collective-permute-done | bytes 524320 | tf_op jit(solution)/shard_map/ppermute | solution.py:19
  16.7 11.8 %collective-permute-done.1.refs_2_ = bf16[128,2048]{1,0:T(8,128)(2,1)S(1)} collective-permute-done((bf16[128,2048]{1,0:T(8,128)(2,1)}, bf16[128,2048]{1,0:T(8,128)(2,1)S(1)}, u32[]{:S(2)}, u32[]{:S(2)}) %collective-permute-start.1) | collective-permute-done | bytes 524320 | tf_op jit(solution)/shard_map/ppermute | solution.py:19
  30.1 10.0 %project.1 = (f32[2,512,512]{2,1,0:T(8,128)}, bf16[512,512]{1,0:T(8,128)(2,1)}, f32[8,512]{1,0:T(8,128)}, bf16[512,2048]{1,0:T(8,128)(2,1)}) custom-call(bf16[128,2048]{1,0:T(8,128)(2,1)} %bitcast.49, bf16[128,2048]{1,0:T(8,128)(2,1)} %copy-done.25, bf16[128,2048]{1,0:T(8,128)(2,1)} %copy-done.26, bf16[128,2048]{1,0:T(8,128)(2,1)} %copy-done.27, ...), custom_call_target="tpu_custom_call" | custom-call | flops 3221225 | bytes 8388 | tf_op jit(solution)/shard_map/project/pallas_call | solution.py:125
  47.5 8.8 %attend.1 = (bf16[512,512]{1,0:T(8,128)(2,1)}, bf16[512,512]{1,0:T(8,128)(2,1)}, bf16[512,512]{1,0:T(8,128)(2,1)}, f32[512,8]{1,0:T(8,128)}, f32[128,2048]{1,0:T...) custom-call(f32[2,512,512]{2,1,0:T(8,128)} %get-tuple-element.74.refs_0_.refs_11_.refs_2_, ...), custom_call_target="tpu_custom_call" | custom-call | flops 1342177 | bytes 7864 | tf_op jit(solution)/shard_map/attend/pallas_call | solution.py:125
  59.8 11.5 %collective-permute-done.6.refs_1_ = bf16[128,2048]{1,0:T(8,128)(2,1)S(1)} collective-permute-done((bf16[128,2048]{1,0:T(8,128)(2,1)}, bf16[128,2048]{1,0:T(8,128)(2,1)S(1)}, u32[]{:S(2)}, u32[]{:S(2)}) %collective-permute-start.6) | collective-permute-done | bytes 524320 | tf_op jit(solution)/shard_map/ppermute | solution.py:19
  71.3 5.9 %collective-permute-done.7.refs_2_ = bf16[128,2048]{1,0:T(8,128)(2,1)S(1)} collective-permute-done((bf16[128,2048]{1,0:T(8,128)(2,1)}, bf16[128,2048]{1,0:T(8,128)(2,1)S(1)}, u32[]{:S(2)}, u32[]{:S(2)}) %collective-permute-start.7) | collective-permute-done | bytes 524320 | tf_op jit(solution)/shard_map/ppermute | solution.py:19
  89.7 16.5 %collective-permute-done.12.refs_0_ = bf16[128,2048]{1,0:T(8,128)(2,1)S(1)} collective-permute-done((bf16[128,2048]{1,0:T(8,128)(2,1)}, bf16[128,2048]{1,0:T(8,128)(2,1)S(1)}, u32[]{:S(2)}, u32[]{:S(2)}) %collective-permute-start.12) | collective-permute-done | bytes 524320 | tf_op jit(solution)/shard_map/ppermute | solution.py:19
  110.5 21.0 %mlp_forward.1 = (bf16[2,512,2048]{2,1,0:T(8,128)(2,1)}, bf16[512,2048]{1,0:T(8,128)(2,1)}, bf16[512,2048]{1,0:T(8,128)(2,1)}, f32[128,2048]{1,0:T(8,128)}, bf16...) custom-call(bf16[128,2048]{1,0:T(8,128)(2,1)} %get-tuple-element.82.refs_0_, ...), custom_call_target="tpu_custom_call" | custom-call | flops 12884901 | bytes 39845 | tf_op jit(solution)/shard_map/mlp_forward/pallas_call | solution.py:125
  136.2 11.5 %collective-permute-done.16.refs_1_ = bf16[128,2048]{1,0:T(8,128)(2,1)S(1)} collective-permute-done((bf16[128,2048]{1,0:T(8,128)(2,1)}, bf16[128,2048]{1,0:T(8,128)(2,1)S(1)}, u32[]{:S(2)}, u32[]{:S(2)}) %collective-permute-start.16) | collective-permute-done | bytes 524320 | tf_op jit(solution)/shard_map/ppermute | solution.py:19
  147.7 8.0 %collective-permute-done.17.refs_2_ = bf16[128,2048]{1,0:T(8,128)(2,1)S(1)} collective-permute-done((bf16[128,2048]{1,0:T(8,128)(2,1)}, bf16[128,2048]{1,0:T(8,128)(2,1)S(1)}, u32[]{:S(2)}, u32[]{:S(2)}) %collective-permute-start.17) | collective-permute-done | bytes 524320 | tf_op jit(solution)/shard_map/ppermute | solution.py:19
  166.4 20.8 %collective-permute-done.25.refs_4_ = bf16[128,2048]{1,0:T(8,128)(2,1)S(1)} collective-permute-done((bf16[128,2048]{1,0:T(8,128)(2,1)}, bf16[128,2048]{1,0:T(8,128)(2,1)S(1)}, u32[]{:S(2)}, u32[]{:S(2)}) %collective-permute-start.25) | collective-permute-done | bytes 524320 | tf_op jit(solution)/shard_map/ppermute | solution.py:19
  192.0 22.5 %mlp_back.1 = (bf16[2,512,2048]{2,1,0:T(8,128)(2,1)}, bf16[512,2048]{1,0:T(8,128)(2,1)}, f32[128,2048]{1,0:T(8,128)}, bf16[128,2048]{1,0:T(8,128)(2,1)}, bf16[12...) custom-call(bf16[128,2048]{1,0:T(8,128)(2,1)} %get-tuple-element.95.refs_0_, bf16[128,2048]{1,0:T(8,128)(2,1)} %copy-done.18, ...), custom_call_target="tpu_custom_call" | custom-call | flops 12884901 | bytes 41943 | tf_op jit(solution)/shard_map/mlp_back/pallas_call | solution.py:125
  219.6 20.6 %mlp_units.1 = (bf16[2,512,2048]{2,1,0:T(8,128)(2,1)}, bf16[512,2048]{1,0:T(8,128)(2,1)}, bf16[512,2048]{1,0:T(8,128)(2,1)}, bf16[512,2048]{1,0:T(8,128)(2,1)}) custom-call(bf16[128,2048]{1,0:T(8,128)(2,1)} %copy-done.13, bf16[128,2048]{1,0:T(8,128)(2,1)} %copy-done, bf16[128,2048]{1,0:T(8,128)(2,1)} %copy-done.1, bf16[128,2048]{1,0:T(8,128)(2,1)} %copy-done.2, ...), custom_call_target="tpu_custom_call" | custom-call | flops 12884901 | bytes 37748 | tf_op jit(solution)/shard_map/mlp_units/pallas_call | solution.py:125
  240.2 14.7 %grad_rows_of.4 = (bf16[512,4096]{1,0:T(8,128)(2,1)}, bf16[256,4096]{1,0:T(8,128)(2,1)}, f32[256,4096]{1,0:T(8,128)}) custom-call(s32[4]{0:T(128)} %broadcast_xor_fusion.1.refs_0_, bf16[512,2048]{1,0:T(8,128)(2,1)} %get-tuple-element.100.refs_1_.refs_2_.refs_3_.refs_4_, bf16[512,2048]{1,0:T(8,128)(2,1)} %get-tuple-element.100.refs_1_.refs_2_.refs_3_.refs_4_, ...), custom_call_target="tpu_custom_call" | custom-call | flops 8589934 | bytes 18874 | tf_op jit(solution)/shard_map/grad_rows_of/pallas_call | solution.py:125
  263.1 9.3 %grad_rows_of.5 = (bf16[512,2048]{1,0:T(8,128)(2,1)}, bf16[256,2048]{1,0:T(8,128)(2,1)}, f32[256,2048]{1,0:T(8,128)}) custom-call(s32[4]{0:T(128)} %broadcast_xor_fusion.1.refs_0_, bf16[512,2048]{1,0:T(8,128)(2,1)} %get-tuple-element.111.refs_1_.refs_2_.refs_3_.refs_4_, bf16[512,2048]{1,0:T(8,128)(2,1)} %get-tuple-element.111.refs_1_.refs_2_.refs_3_.refs_4_, ...), custom_call_target="tpu_custom_call" | custom-call | flops 429496729600 | bytes 1048576000 | tf_op jit(solution)/shard_map/grad_rows_of/pallas_call | solution.py:125
  280.0 5.5 %collective-permute-done.30.refs_2_ = bf16[128,2048]{1,0:T(8,128)(2,1)} collective-permute-done((bf16[128,2048]{1,0:T(8,128)(2,1)}, bf16[128,2048]{1,0:T(8,128)(2,1)}, u32[]{:S(2)}, u32[]{:S(2)}) %collective-permute-start.30) | collective-permute-done | bytes 524320 | tf_op jit(solution)/shard_map/ppermute | solution.py:19
  285.5 11.6 %attend_back.1 = (bf16[512,2048]{1,0:T(8,128)(2,1)}, f32[2,512,512]{2,1,0:T(8,128)}, bf16[512,512]{1,0:T(8,128)(2,1)}, f32[8,512]{1,0:T(8,128)}, f32[2,512]{1,0:T(2,128)}) custom-call(bf16[128,2048]{1,0:T(8,128)(2,1)} %get-tuple-element.106.refs_0_, bf16[128,2048]{1,0:T(8,128)(2,1)} %collective-permute-done.29.refs_1_, ...), custom_call_target="tpu_custom_call" | custom-call | flops 174483046400 | bytes 1048576000 | tf_op jit(solution)/shard_map/attend_back/pallas_call | solution.py:125
  307.8 10.1 %project_back.1 = (bf16[3,512,512]{2,1,0:T(8,128)(2,1)}, f32[128,2048]{1,0:T(8,128)}, bf16[128,2048]{1,0:T(8,128)(2,1)}, bf16[128,2048]{1,0:T(8,128)(2,1)}, bf16[128,2048]{1,0:T(8,128)(2,1)}) custom-call(f32[2,512,512]{2,1,0:T(8,128)} %get-tuple-element.116.refs_0_, bf16[512,512]{1,0:T(8,128)(2,1)} %get-tuple-element.117.refs_1_, ...), custom_call_target="tpu_custom_call" | custom-call | flops 3221225 | bytes 14155 | tf_op jit(solution)/shard_map/project_back/pallas_call | solution.py:125
  328.0 8.1 %grad_rows_of.6 = (bf16[1024,1536]{1,0:T(8,128)(2,1)}, bf16[512,1536]{1,0:T(8,128)(2,1)}, bf16[256,1536]{1,0:T(8,128)(2,1)}, f32[256,1536]{1,0:T(8,128)}) custom-call(s32[8]{0:T(128)} %broadcast_xor_fusion.refs_0_, bf16[512,2048]{1,0:T(8,128)(2,1)} %get-tuple-element.125.refs_1_.refs_2_.refs_3_.refs_4_.refs_5_.refs_6_.refs_7_.refs_8_, ...), custom_call_target="tpu_custom_call" | custom-call | flops 3221225 | bytes 9961 | tf_op jit(solution)/shard_map/grad_rows_of/pallas_call | solution.py:125
  361.4 5.8 %OwnersSum_finish.4.refs_3_ = f32[2,256,2048]{2,1,0:T(8,128)} custom-call(f32[256,4096]{1,0:T(8,128)} %get-tuple-element.135.refs_0_, bf16[512,4096]{1,0:T(8,128)(2,1)} %collective-permute-done.32.refs_1_.refs_3_, bf16[256,2048]{1,0:T(8,128)(2,1)} %collective-permute-done.37.refs_11_.refs_2_, bf16[512,4096]{1,0:T(8,128)(2,1)} %collective-permute-done.32.refs_1_.refs_3_, ...), custom_call_target="tpu_custom_call" | custom-call | flops 4194 | bytes 12582 | tf_op jit(solution)/shard_map/OwnersSum_finish/pallas_call | solution.py:125
  374.4 8.5 %collective-permute-done.51.refs_2_.refs_5_ = bf16[512,512]{1,0:T(8,128)(2,1)S(1)} collective-permute-done((bf16[512,512]{1,0:T(8,128)(2,1)}, bf16[512,512]{1,0:T(8,128)(2,1)S(1)}, u32[]{:S(2)}, u32[]{:S(2)}) %collective-permute-start.51) | collective-permute-done | bytes 524320 | tf_op jit(solution)/shard_map/ppermute | solution.py:19
  385.6 14.1 %collective-permute-done.53.refs_2_.refs_8_ = bf16[512,512]{1,0:T(8,128)(2,1)S(1)} collective-permute-done((bf16[512,512]{1,0:T(8,128)(2,1)}, bf16[512,512]{1,0:T(8,128)(2,1)S(1)}, u32[]{:S(2)}, u32[]{:S(2)}) %collective-permute-start.53) | collective-permute-done | bytes 524320 | tf_op jit(solution)/shard_map/ppermute | solution.py:19
  399.7 5.0 %collective-permute-done.50.refs_4_.refs_3_ = bf16[256,512]{1,0:T(8,128)(2,1)S(1)} collective-permute-done((bf16[256,512]{1,0:T(8,128)(2,1)}, bf16[256,512]{1,0:T(8,128)(2,1)S(1)}, u32[]{:S(2)}, u32[]{:S(2)}) %collective-permute-start.50) | collective-permute-done | bytes 262176 | tf_op jit(solution)/shard_map/ppermute | solution.py:19
  422.7 11.5 %collective-permute-done.54.refs_9_ = bf16[256,512]{1,0:T(8,128)(2,1)S(1)} collective-permute-done((bf16[256,512]{1,0:T(8,128)(2,1)S(1)}, bf16[256,512]{1,0:T(8,128)(2,1)S(1)}, u32[]{:S(2)}, u32[]{:S(2)}) %collective-permute-start.54) | collective-permute-done | bytes 262176 | tf_op jit(solution)/shard_map/ppermute | solution.py:19
  (264 shorter events, 164.0 us)
Async XLA Ops:
  3.7 24.8 %collective-permute-start.1 = (bf16[128,2048]{1,0:T(8,128)(2,1)}, bf16[128,2048]{1,0:T(8,128)(2,1)S(1)}, u32[]{:S(2)}, u32[]{:S(2)}) collective-permute-start(bf16[128,2048]{1,0:T(8,128)(2,1)} %bitcast.47), channel_id=1, source_target_pairs={{0,2},{1,3},{2,0},{3,1},{4,6},{5,7},{6,4},{7,5},{8,10},{9,11},{10,... | collective-permute-start | bytes 1572872 | tf_op jit(solution)/shard_map/ppermute | solution.py:19
  106.3 25.3 %collective-permute-start.13 = (bf16[128,2048]{1,0:T(8,128)(2,1)S(1)}, bf16[128,2048]{1,0:T(8,128)(2,1)S(1)}, u32[]{:S(2)}, u32[]{:S(2)}) collective-permute-start(bf16[128,2048]{1,0:T(8,128)(2,1)S(1)} %collective-permute-done.12.refs_0_), channel_id=1, source_target_pairs={{0,1},{1,0},{2,3},{3,2},{4,5},{5,4},{6,7},{7,6},{8,9},{9,8},{10,11... | collective-permute-start | bytes 1572872 | tf_op jit(solution)/shard_map/ppermute | solution.py:19
  106.3 25.3 %collective-permute-start.14 = (bf16[128,2048]{1,0:T(8,128)(2,1)S(1)}, bf16[128,2048]{1,0:T(8,128)(2,1)S(1)}, u32[]{:S(2)}, u32[]{:S(2)}) collective-permute-start(bf16[128,2048]{1,0:T(8,128)(2,1)S(1)} %collective-permute-done.12.refs_0_), channel_id=1, source_target_pairs={{0,2},{1,3},{2,0},{3,1},{4,6},{5,7},{6,4},{7,5},{8,10},{9,11},{10,... | collective-permute-start | bytes 1572872 | tf_op jit(solution)/shard_map/ppermute | solution.py:19
  162.7 24.5 %collective-permute-start.25 = (bf16[128,2048]{1,0:T(8,128)(2,1)}, bf16[128,2048]{1,0:T(8,128)(2,1)S(1)}, u32[]{:S(2)}, u32[]{:S(2)}) collective-permute-start(bf16[128,2048]{1,0:T(8,128)(2,1)} %get-tuple-element.95.refs_0_), channel_id=1, source_target_pairs={{0,16},{4,20},{8,24},{12,28},{16,0},{20,4},{24,8},{28,12},{1,17},{... | collective-permute-start | bytes 1572872 | tf_op jit(solution)/shard_map/ppermute | solution.py:19
  162.8 24.7 %collective-permute-start.19 = (bf16[128,2048]{1,0:T(8,128)(2,1)}, bf16[128,2048]{1,0:T(8,128)(2,1)S(1)}, u32[]{:S(2)}, u32[]{:S(2)}) collective-permute-start(bf16[128,2048]{1,0:T(8,128)(2,1)} %get-tuple-element.95.refs_0_), channel_id=1, source_target_pairs={{0,1},{1,0},{2,3},{3,2},{4,5},{5,4},{6,7},{7,6},{8,9},{9,8},{10,11... | collective-permute-start | bytes 1572872 | tf_op jit(solution)/shard_map/ppermute | solution.py:19
  163.7 27.5 %collective-permute-start.20 = (bf16[128,2048]{1,0:T(8,128)(2,1)}, bf16[128,2048]{1,0:T(8,128)(2,1)S(1)}, u32[]{:S(2)}, u32[]{:S(2)}) collective-permute-start(bf16[128,2048]{1,0:T(8,128)(2,1)} %get-tuple-element.95.refs_0_), channel_id=1, source_target_pairs={{0,2},{1,3},{2,0},{3,1},{4,6},{5,7},{6,4},{7,5},{8,10},{9,11},{10,... | collective-permute-start | bytes 1572872 | tf_op jit(solution)/shard_map/ppermute | solution.py:19
  165.4 25.8 %collective-permute-start.21 = (bf16[128,2048]{1,0:T(8,128)(2,1)}, bf16[128,2048]{1,0:T(8,128)(2,1)}, u32[]{:S(2)}, u32[]{:S(2)}) collective-permute-start(bf16[128,2048]{1,0:T(8,128)(2,1)} %get-tuple-element.95.refs_0_), channel_id=1, source_target_pairs={{0,3},{1,2},{2,1},{3,0},{4,7},{5,6},{6,5},{7,4},{8,11},{9,10},{10,... | collective-permute-start | bytes 1572872 | tf_op jit(solution)/shard_map/ppermute | solution.py:19
  187.2 28.0 %collective-permute-start.26 = (bf16[128,2048]{1,0:T(8,128)(2,1)S(1)}, bf16[128,2048]{1,0:T(8,128)(2,1)S(1)}, u32[]{:S(2)}, u32[]{:S(2)}) collective-permute-start(bf16[128,2048]{1,0:T(8,128)(2,1)S(1)} %collective-permute-done.25.refs_4_), channel_id=1, source_target_pairs={{0,1},{1,0},{2,3},{3,2},{4,5},{5,4},{6,7},{7,6},{8,9},{9,8},{10,11... | collective-permute-start | bytes 1572872 | tf_op jit(solution)/shard_map/ppermute | solution.py:19
  187.5 30.6 %collective-permute-start.27 = (bf16[128,2048]{1,0:T(8,128)(2,1)S(1)}, bf16[128,2048]{1,0:T(8,128)(2,1)S(1)}, u32[]{:S(2)}, u32[]{:S(2)}) collective-permute-start(bf16[128,2048]{1,0:T(8,128)(2,1)S(1)} %collective-permute-done.25.refs_4_), channel_id=1, source_target_pairs={{0,2},{1,3},{2,0},{3,1},{4,6},{5,7},{6,4},{7,5},{8,10},{9,11},{10,... | collective-permute-start | bytes 1572872 | tf_op jit(solution)/shard_map/ppermute | solution.py:19
  187.5 30.6 %collective-permute-start.28 = (bf16[128,2048]{1,0:T(8,128)(2,1)S(1)}, bf16[128,2048]{1,0:T(8,128)(2,1)S(1)}, u32[]{:S(2)}, u32[]{:S(2)}) collective-permute-start(bf16[128,2048]{1,0:T(8,128)(2,1)S(1)} %collective-permute-done.25.refs_4_), channel_id=1, source_target_pairs={{0,3},{1,2},{2,1},{3,0},{4,7},{5,6},{6,5},{7,4},{8,11},{9,10},{10,... | collective-permute-start | bytes 1572872 | tf_op jit(solution)/shard_map/ppermute | solution.py:19
  214.5 40.5 %collective-permute-start.22 = (bf16[128,2048]{1,0:T(8,128)(2,1)}, bf16[128,2048]{1,0:T(8,128)(2,1)}, u32[]{:S(2)}, u32[]{:S(2)}) collective-permute-start(bf16[128,2048]{1,0:T(8,128)(2,1)} %get-tuple-element.97), channel_id=1, source_target_pairs={{0,1},{1,0},{2,3},{3,2},{4,5},{5,4},{6,7},{7,6},{8,9},{9,8},{10,11... | collective-permute-start | bytes 1572872 | tf_op jit(solution)/shard_map/ppermute | solution.py:19
  214.8 40.1 %collective-permute-start.23 = (bf16[128,2048]{1,0:T(8,128)(2,1)}, bf16[128,2048]{1,0:T(8,128)(2,1)}, u32[]{:S(2)}, u32[]{:S(2)}) collective-permute-start(bf16[128,2048]{1,0:T(8,128)(2,1)} %get-tuple-element.98), channel_id=1, source_target_pairs={{0,2},{1,3},{2,0},{3,1},{4,6},{5,7},{6,4},{7,5},{8,10},{9,11},{10,... | collective-permute-start | bytes 1572872 | tf_op jit(solution)/shard_map/ppermute | solution.py:19
  215.2 39.8 %collective-permute-start.24 = (bf16[128,2048]{1,0:T(8,128)(2,1)}, bf16[128,2048]{1,0:T(8,128)(2,1)}, u32[]{:S(2)}, u32[]{:S(2)}) collective-permute-start(bf16[128,2048]{1,0:T(8,128)(2,1)} %get-tuple-element.99), channel_id=1, source_target_pairs={{0,3},{1,2},{2,1},{3,0},{4,7},{5,6},{6,5},{7,4},{8,11},{9,10},{10,... | collective-permute-start | bytes 1572872 | tf_op jit(solution)/shard_map/ppermute | solution.py:19
  259.8 25.7 %collective-permute-start.30 = (bf16[128,2048]{1,0:T(8,128)(2,1)}, bf16[128,2048]{1,0:T(8,128)(2,1)}, u32[]{:S(2)}, u32[]{:S(2)}) collective-permute-start(bf16[128,2048]{1,0:T(8,128)(2,1)} %get-tuple-element.106.refs_0_), channel_id=1, source_target_pairs={{0,2},{1,3},{2,0},{3,1},{4,6},{5,7},{6,4},{7,5},{8,10},{9,11},{10,... | collective-permute-start | bytes 1572872 | tf_op jit(solution)/shard_map/ppermute | solution.py:19
  260.3 25.2 %collective-permute-start.31 = (bf16[128,2048]{1,0:T(8,128)(2,1)}, bf16[128,2048]{1,0:T(8,128)(2,1)}, u32[]{:S(2)}, u32[]{:S(2)}) collective-permute-start(bf16[128,2048]{1,0:T(8,128)(2,1)} %get-tuple-element.106.refs_0_), channel_id=1, source_target_pairs={{0,3},{1,2},{2,1},{3,0},{4,7},{5,6},{6,5},{7,4},{8,11},{9,10},{10,... | collective-permute-start | bytes 1572872 | tf_op jit(solution)/shard_map/ppermute | solution.py:19
  272.4 26.7 %collective-permute-start.36 = (bf16[512,2048]{1,0:T(8,128)(2,1)}, bf16[512,2048]{1,0:T(8,128)(2,1)}, u32[]{:S(2)}, u32[]{:S(2)}) collective-permute-start(bf16[512,2048]{1,0:T(8,128)(2,1)} %get-tuple-element.115.refs_2_), channel_id=1, source_target_pairs={{0,4},{4,0},{8,12},{12,8},{16,20},{20,16},{24,28},{28,24},{1,5},{5... | collective-permute-start | bytes 6291464 | tf_op jit(solution)/shard_map/ppermute | solution.py:19
  275.2 32.1 %collective-permute-start.37 = (bf16[256,2048]{1,0:T(8,128)(2,1)}, bf16[256,2048]{1,0:T(8,128)(2,1)}, u32[]{:S(2)}, u32[]{:S(2)}) collective-permute-start(bf16[256,2048]{1,0:T(8,128)(2,1)} %add_parts.11.refs_2_), channel_id=1, source_target_pairs={{0,8},{4,12},{8,0},{12,4},{16,24},{20,28},{24,16},{28,20},{1,9},{5... | collective-permute-start | bytes 3145736 | tf_op jit(solution)/shard_map/ppermute | solution.py:19
  280.0 47.4 %collective-permute-start.41 = (bf16[256,2048]{1,0:T(8,128)(2,1)}, bf16[256,2048]{1,0:T(8,128)(2,1)}, u32[]{:S(2)}, u32[]{:S(2)}) collective-permute-start(bf16[256,2048]{1,0:T(8,128)(2,1)} %add_parts.12.refs_14_), channel_id=1, source_target_pairs={{0,8},{4,12},{8,0},{12,4},{16,24},{20,28},{24,16},{28,20},{1,9},{5... | collective-permute-start | bytes 3145736 | tf_op jit(solution)/shard_map/ppermute | solution.py:19
  303.5 42.7 %collective-permute-start.43 = (bf16[256,2048]{1,0:T(8,128)(2,1)}, bf16[256,2048]{1,0:T(8,128)(2,1)S(1)}, u32[]{:S(2)}, u32[]{:S(2)}) collective-permute-start(bf16[256,2048]{1,0:T(8,128)(2,1)} %add_parts.13.refs_10_), channel_id=1, source_target_pairs={{0,8},{4,12},{8,0},{12,4},{16,24},{20,28},{24,16},{28,20},{1,9},{5... | collective-permute-start | bytes 3145736 | tf_op jit(solution)/shard_map/ppermute | solution.py:19
  354.9 28.0 %collective-permute-start.51 = (bf16[512,512]{1,0:T(8,128)(2,1)}, bf16[512,512]{1,0:T(8,128)(2,1)S(1)}, u32[]{:S(2)}, u32[]{:S(2)}) collective-permute-start(bf16[512,512]{1,0:T(8,128)(2,1)} %add_parts.15.refs_2_), channel_id=1, source_target_pairs={{0,8},{4,12},{8,0},{12,4},{16,24},{20,28},{24,16},{28,20},{1,9},{5... | collective-permute-start | bytes 1572872 | tf_op jit(solution)/shard_map/ppermute | solution.py:19
  357.3 42.4 %collective-permute-start.53 = (bf16[512,512]{1,0:T(8,128)(2,1)}, bf16[512,512]{1,0:T(8,128)(2,1)S(1)}, u32[]{:S(2)}, u32[]{:S(2)}) collective-permute-start(bf16[512,512]{1,0:T(8,128)(2,1)} %add_parts.16.refs_2_), channel_id=1, source_target_pairs={{0,8},{4,12},{8,0},{12,4},{16,24},{20,28},{24,16},{28,20},{1,9},{5... | collective-permute-start | bytes 1572872 | tf_op jit(solution)/shard_map/ppermute | solution.py:19
  361.1 49.0 %collective-permute-start.55 = (bf16[512,512]{1,0:T(8,128)(2,1)}, bf16[512,512]{1,0:T(8,128)(2,1)S(1)}, u32[]{:S(2)}, u32[]{:S(2)}) collective-permute-start(bf16[512,512]{1,0:T(8,128)(2,1)} %add_parts.17.refs_5_), channel_id=1, source_target_pairs={{0,8},{4,12},{8,0},{12,4},{16,24},{20,28},{24,16},{28,20},{1,9},{5... | collective-permute-start | bytes 1572872 | tf_op jit(solution)/shard_map/ppermute | solution.py:19
  369.9 34.8 %collective-permute-start.50 = (bf16[256,512]{1,0:T(8,128)(2,1)}, bf16[256,512]{1,0:T(8,128)(2,1)S(1)}, u32[]{:S(2)}, u32[]{:S(2)}) collective-permute-start(bf16[256,512]{1,0:T(8,128)(2,1)} %add_parts.18.refs_3_), channel_id=1, source_target_pairs={{0,16},{4,20},{8,24},{12,28},{16,0},{20,4},{24,8},{28,12},{1,17},{... | collective-permute-start | bytes 786440 | tf_op jit(solution)/shard_map/ppermute | solution.py:19
  385.6 24.6 %collective-permute-start.52 = (bf16[256,512]{1,0:T(8,128)(2,1)}, bf16[256,512]{1,0:T(8,128)(2,1)S(1)}, u32[]{:S(2)}, u32[]{:S(2)}) collective-permute-start(bf16[256,512]{1,0:T(8,128)(2,1)} %add_parts.19.refs_3_), channel_id=1, source_target_pairs={{0,16},{4,20},{8,24},{12,28},{16,0},{20,4},{24,8},{28,12},{1,17},{... | collective-permute-start | bytes 786440 | tf_op jit(solution)/shard_map/ppermute | solution.py:19
  (85 other events, 796.1 us)
where the time goes:
time: 446 us; the launch traced here: 444 us
  Pallas kernels  197 us (44%)
  waiting for transfers between devices  153 us (34%)
  starting transfers between devices  62.9 us (14%)
  local copies, waits for them, and re-layouts  16.5 us (4%)
  other arithmetic  10.9 us (2%)
    pallas_call x35, Pallas kernels, launch(): results = pl.pallas_call(body, **settings)(*args, *waits)  197 us
    ppermute x59, waiting for transfers between devices, exchange(): return lax.ppermute(value, axis, [(i, i ^ flip) for i in range(size)])  153 us
    ppermute x59, starting transfers between devices, exchange(): return lax.ppermute(value, axis, [(i, i ^ flip) for i in range(size)])  62.9 us
    unnamed x100, local copies, waits for them, and re-layouts  15 us
  transfers between devices with their start and end apart: 59, of which 23 were waited for; matrix products, arithmetic and copies ran while one was open for 3% of the time, Pallas kernels for 38%

commit v1 on v0

--- a/solution.py
+++ b/solution.py
@@ -162,7 +162,7 @@
     )
 
 
-def project(order, x_blocks, qkv_weight):
+def project(order, x_blocks, qkv_weight, part, parts, begun):
     count = len(x_blocks)
     tok, model_width = x_blocks[0].shape
     rows = count * tok
@@ -170,7 +170,8 @@
 
     def kernel(*refs):
         x_refs = refs[:count]
-        weight_ref, raw_ref, values_ref, squares_ref, x_ref = refs[count:]
+        weight_ref = refs[count]
+        raw_ref, values_ref, squares_ref, x_ref = refs[-4:]
         step = pl.program_id(0)
 
         @pl.when(step == 0)
@@ -193,21 +194,24 @@
     return launch(
         order,
         kernel,
-        [*x_blocks, qkv_weight],
+        [*x_blocks, qkv_weight, *begun],
         out_shape=[
-            shape((2, rows, width), F32),
-            shape((rows, width), BF),
-            shape((8, rows), F32),
-            shape((rows, model_width), BF),
+            shape((2, parts * rows, width), F32),
+            shape((parts * rows, width), BF),
+            shape((8, parts * rows), F32),
+            shape((parts * rows, model_width), BF),
         ],
         grid=(3,),
-        in_specs=[whole] * count + [pl.BlockSpec((None, model_width, width), lambda n: (n, 0, 0))],
+        in_specs=[whole] * count
+        + [pl.BlockSpec((None, model_width, width), lambda n: (n, 0, 0))]
+        + [pl.BlockSpec(memory_space=pl.ANY)] * len(begun),
         out_specs=[
-            pl.BlockSpec((None, rows, width), lambda n: (jnp.minimum(n, 1), 0, 0)),
-            pl.BlockSpec((rows, width), lambda n: (0, 0)),
-            pl.BlockSpec((8, rows), lambda n: (0, 0)),
-            pl.BlockSpec((rows, model_width), lambda n: (0, 0)),
+            pl.BlockSpec((None, rows, width), lambda n: (jnp.minimum(n, 1), part, 0)),
+            pl.BlockSpec((rows, width), lambda n: (part, 0)),
+            pl.BlockSpec((8, rows), lambda n: (0, part)),
+            pl.BlockSpec((rows, model_width), lambda n: (part, 0)),
         ],
+        input_output_aliases={count + 1 + k: k for k in range(len(begun))},
         compiler_params=WHOLE,
         cost_estimate=cost(6 * rows * model_width * width, 6 * model_width * width + 8 * rows * width),
     )
@@ -995,7 +999,10 @@
     order = Order()
     x_blocks = gather_blocks(x_rows)
     tables = jax.vmap(tree_tables, in_axes=(0, 0, None))(parents[:, 0], lengths[:, 0], places)
-    raw, values, squares, x_full = project(order, x_blocks, qkv_weight)
+    half = size // 2
+    begun = project(order, x_blocks[:half], qkv_weight, 0, 2, [])
+    order.clear()
+    raw, values, squares, x_full = project(order, x_blocks[half:], qkv_weight, 1, 2, begun)
     context, queries, keys, inv, *attn_blocks = attend(
         order, raw, values, gather_blocks(squares), tables, qk_gain, out_weight
     )
@@ -1023,16 +1030,20 @@
     gate_up_sum = OwnersSum(
         order, [(hidden_full, d_gate_up, 0, rows), (far_hidden, far_d_gate_up, 0, rows)], far, 2
     )
+    order.pace = 1000000
     d_hidden, d_attn, attn_gain_sum = before_attention(
         order, d_hidden_parts, grad_rows, attn, post_gain
     )
     d_attn_blocks = gather_blocks(d_attn)
+    order.pace = 0.001
+    gate_up_sum.at += 1
+    gate_up_sum.send(order, 0)
     order.pace = 100
     down_sum = OwnersSum(
         order, [(d_mlp_full, swiglu[None], 0, rows), (far_d_mlp, far_swiglu[None], 0, rows)], far
     )
     order.pace = 0.001
-    gate_up_sum.step(order)
+    gate_up_sum.send(order, 1)
     order.pace = 100
     d_attn_full, d_norm, d_values, sums, qk_gain_sums = attend_back(
         order, d_attn_blocks, out_weight, queries, keys, values, raw, inv, tables, qk_gain

time: 446 us -> 439 us (0.984)
  waiting for transfers between devices: 153 us -> 144 us
    ppermute x59, waiting for transfers between devices: 153 us -> 144 us  [exchange(): return lax.ppermute(value, axis, [(i, i ^ flip) for i in range(size)])]
    pallas_call x35 -> x36, Pallas kernels: 197 us -> 201 us  [launch(): results = pl.pallas_call(body, **settings)(*args, *waits)]
    unnamed x100 -> x96, local copies, waits for them, and re-layouts: 15 us -> 15.2 us
  transfers between devices with their start and end apart: 59 -> 59, of which waited for: 23 -> 24; matrix products, arithmetic and copies ran while one was open for 3% -> 3% of each run, Pallas kernels for 38% -> 40%
where the time goes in v1:
time: 439 us; the launch traced here: 438 us
  Pallas kernels  201 us (46%)
  waiting for transfers between devices  144 us (33%)
  starting transfers between devices  61.8 us (14%)
  local copies, waits for them, and re-layouts  16.6 us (4%)
  other arithmetic  11.5 us (3%)
    pallas_call x36, Pallas kernels, launch(): results = pl.pallas_call(body, **settings)(*args, *waits)  201 us
    ppermute x59, waiting for transfers between devices, exchange(): return lax.ppermute(value, axis, [(i, i ^ flip) for i in range(size)])  144 us
    ppermute x59, starting transfers between devices, exchange(): return lax.ppermute(value, axis, [(i, i ^ flip) for i in range(size)])  61.8 us
    unnamed x96, local copies, waits for them, and re-layouts  15.2 us
  transfers between devices with their start and end apart: 59, of which 24 were waited for; matrix products, arithmetic and copies ran while one was open for 3% of the time, Pallas kernels for 40%

profile of v1, /device:TPU:0, one launch (start us, length us, event | category | flops | bytes accessed | tf_op | source)
XLA Modules:
  0.0 437.8 jit_solution(2898860075558521084)
XLA Ops:
  10.9 5.7 %collective-permute-done.2.refs_1_ = bf16[128,2048]{1,0:T(8,128)(2,1)S(1)} collective-permute-done((bf16[128,2048]{1,0:T(8,128)(2,1)}, bf16[128,2048]{1,0:T(8,128)(2,1)S(1)}, u32[]{:S(2)}, u32[]{:S(2)}) %collective-permute-start.2) | collective-permute-done | bytes 524320 | tf_op jit(solution)/shard_map/ppermute | solution.py:19
  17.4 7.0 %project.2 = (f32[2,512,512]{2,1,0:T(8,128)}, bf16[512,512]{1,0:T(8,128)(2,1)}, f32[8,512]{1,0:T(8,128)}, bf16[512,2048]{1,0:T(8,128)(2,1)}) custom-call(bf16[128,2048]{1,0:T(8,128)(2,1)} %bitcast.49, bf16[128,2048]{1,0:T(8,128)(2,1)} %copy-done.22, bf16[3,2048,512]{2,1,0:T(8,128)(2,1)} %refs_5_.7), custom_call_target="tpu_custom_call" | custom-call | flops 1610612 | bytes 7340 | tf_op jit(solution)/shard_map/project/pallas_call | solution.py:125
  29.5 6.9 %project.3 = (f32[2,512,512]{2,1,0:T(8,128)}, bf16[512,512]{1,0:T(8,128)(2,1)}, f32[8,512]{1,0:T(8,128)}, bf16[512,2048]{1,0:T(8,128)(2,1)}) custom-call(bf16[128,2048]{1,0:T(8,128)(2,1)} %copy-done.26, bf16[128,2048]{1,0:T(8,128)(2,1)} %copy-done.27, ...), custom_call_target="tpu_custom_call", output_to_operand_aliasing={{0}: (3, {}), {1}: (4, {}), {2}: (5, {}), {3}: (6, {})} | custom-call | flops 1610612 | bytes 7340 | tf_op jit(solution)/shard_map/project/pallas_call | solution.py:125
  43.9 8.8 %attend.1 = (bf16[512,512]{1,0:T(8,128)(2,1)}, bf16[512,512]{1,0:T(8,128)(2,1)}, bf16[512,512]{1,0:T(8,128)(2,1)}, f32[512,8]{1,0:T(8,128)}, f32[128,2048]{1,0:T...) custom-call(f32[2,512,512]{2,1,0:T(8,128)} %get-tuple-element.82.refs_0_.refs_11_.refs_2_, ...), custom_call_target="tpu_custom_call" | custom-call | flops 1342177 | bytes 7864 | tf_op jit(solution)/shard_map/attend/pallas_call | solution.py:125
  56.2 11.5 %collective-permute-done.6.refs_1_ = bf16[128,2048]{1,0:T(8,128)(2,1)S(1)} collective-permute-done((bf16[128,2048]{1,0:T(8,128)(2,1)}, bf16[128,2048]{1,0:T(8,128)(2,1)S(1)}, u32[]{:S(2)}, u32[]{:S(2)}) %collective-permute-start.6) | collective-permute-done | bytes 524320 | tf_op jit(solution)/shard_map/ppermute | solution.py:19
  67.7 6.5 %collective-permute-done.7.refs_2_ = bf16[128,2048]{1,0:T(8,128)(2,1)S(1)} collective-permute-done((bf16[128,2048]{1,0:T(8,128)(2,1)}, bf16[128,2048]{1,0:T(8,128)(2,1)S(1)}, u32[]{:S(2)}, u32[]{:S(2)}) %collective-permute-start.7) | collective-permute-done | bytes 524320 | tf_op jit(solution)/shard_map/ppermute | solution.py:19
  86.8 16.7 %collective-permute-done.12.refs_0_ = bf16[128,2048]{1,0:T(8,128)(2,1)S(1)} collective-permute-done((bf16[128,2048]{1,0:T(8,128)(2,1)}, bf16[128,2048]{1,0:T(8,128)(2,1)S(1)}, u32[]{:S(2)}, u32[]{:S(2)}) %collective-permute-start.12) | collective-permute-done | bytes 524320 | tf_op jit(solution)/shard_map/ppermute | solution.py:19
  107.8 21.0 %mlp_forward.1 = (bf16[2,512,2048]{2,1,0:T(8,128)(2,1)}, bf16[512,2048]{1,0:T(8,128)(2,1)}, bf16[512,2048]{1,0:T(8,128)(2,1)}, f32[128,2048]{1,0:T(8,128)}, bf16...) custom-call(bf16[128,2048]{1,0:T(8,128)(2,1)} %get-tuple-element.90.refs_0_, ...), custom_call_target="tpu_custom_call" | custom-call | flops 12884901 | bytes 39845 | tf_op jit(solution)/shard_map/mlp_forward/pallas_call | solution.py:125
  133.5 11.5 %collective-permute-done.16.refs_1_ = bf16[128,2048]{1,0:T(8,128)(2,1)S(1)} collective-permute-done((bf16[128,2048]{1,0:T(8,128)(2,1)}, bf16[128,2048]{1,0:T(8,128)(2,1)S(1)}, u32[]{:S(2)}, u32[]{:S(2)}) %collective-permute-start.16) | collective-permute-done | bytes 524320 | tf_op jit(solution)/shard_map/ppermute | solution.py:19
  145.0 8.0 %collective-permute-done.17.refs_2_ = bf16[128,2048]{1,0:T(8,128)(2,1)S(1)} collective-permute-done((bf16[128,2048]{1,0:T(8,128)(2,1)}, bf16[128,2048]{1,0:T(8,128)(2,1)S(1)}, u32[]{:S(2)}, u32[]{:S(2)}) %collective-permute-start.17) | collective-permute-done | bytes 524320 | tf_op jit(solution)/shard_map/ppermute | solution.py:19
  163.6 20.8 %collective-permute-done.25.refs_4_ = bf16[128,2048]{1,0:T(8,128)(2,1)S(1)} collective-permute-done((bf16[128,2048]{1,0:T(8,128)(2,1)}, bf16[128,2048]{1,0:T(8,128)(2,1)S(1)}, u32[]{:S(2)}, u32[]{:S(2)}) %collective-permute-start.25) | collective-permute-done | bytes 524320 | tf_op jit(solution)/shard_map/ppermute | solution.py:19
  189.2 22.5 %mlp_back.1 = (bf16[2,512,2048]{2,1,0:T(8,128)(2,1)}, bf16[512,2048]{1,0:T(8,128)(2,1)}, f32[128,2048]{1,0:T(8,128)}, bf16[128,2048]{1,0:T(8,128)(2,1)}, bf16[12...) custom-call(bf16[128,2048]{1,0:T(8,128)(2,1)} %get-tuple-element.103.refs_0_, bf16[128,2048]{1,0:T(8,128)(2,1)} %copy-done.18, ...), custom_call_target="tpu_custom_call" | custom-call | flops 12884901 | bytes 41943 | tf_op jit(solution)/shard_map/mlp_back/pallas_call | solution.py:125
  216.8 20.6 %mlp_units.1 = (bf16[2,512,2048]{2,1,0:T(8,128)(2,1)}, bf16[512,2048]{1,0:T(8,128)(2,1)}, bf16[512,2048]{1,0:T(8,128)(2,1)}, bf16[512,2048]{1,0:T(8,128)(2,1)}) custom-call(bf16[128,2048]{1,0:T(8,128)(2,1)} %copy-done.13, bf16[128,2048]{1,0:T(8,128)(2,1)} %copy-done.1, bf16[128,2048]{1,0:T(8,128)(2,1)} %copy-done.2, bf16[128,2048]{1,0:T(8,128)(2,1)} %copy-done.3, ...), custom_call_target="tpu_custom_call" | custom-call | flops 12884901 | bytes 37748 | tf_op jit(solution)/shard_map/mlp_units/pallas_call | solution.py:125
  237.4 14.7 %grad_rows_of.4 = (bf16[512,4096]{1,0:T(8,128)(2,1)}, bf16[256,4096]{1,0:T(8,128)(2,1)}, f32[256,4096]{1,0:T(8,128)}) custom-call(s32[4]{0:T(128)} %broadcast_xor_fusion.1.refs_0_, bf16[512,2048]{1,0:T(8,128)(2,1)} %get-tuple-element.108.refs_1_.refs_2_.refs_3_.refs_4_, bf16[512,2048]{1,0:T(8,128)(2,1)} %get-tuple-element.108.refs_1_.refs_2_.refs_3_.refs_4_, ...), custom_call_target="tpu_custom_call" | custom-call | flops 8589934 | bytes 18874 | tf_op jit(solution)/shard_map/grad_rows_of/pallas_call | solution.py:125
  265.1 9.3 %grad_rows_of.5 = (bf16[512,2048]{1,0:T(8,128)(2,1)}, bf16[256,2048]{1,0:T(8,128)(2,1)}, f32[256,2048]{1,0:T(8,128)}) custom-call(s32[4]{0:T(128)} %broadcast_xor_fusion.1.refs_0_, bf16[512,2048]{1,0:T(8,128)(2,1)} %get-tuple-element.119.refs_1_.refs_2_.refs_3_.refs_4_, bf16[512,2048]{1,0:T(8,128)(2,1)} %get-tuple-element.119.refs_1_.refs_2_.refs_3_.refs_4_, ...), custom_call_target="tpu_custom_call" | custom-call | flops 429496729600 | bytes 1048576000 | tf_op jit(solution)/shard_map/grad_rows_of/pallas_call | solution.py:125
  277.2 5.5 %collective-permute-done.30.refs_2_ = bf16[128,2048]{1,0:T(8,128)(2,1)} collective-permute-done((bf16[128,2048]{1,0:T(8,128)(2,1)}, bf16[128,2048]{1,0:T(8,128)(2,1)}, u32[]{:S(2)}, u32[]{:S(2)}) %collective-permute-start.30) | collective-permute-done | bytes 524320 | tf_op jit(solution)/shard_map/ppermute | solution.py:19
  282.6 11.6 %attend_back.1 = (bf16[512,2048]{1,0:T(8,128)(2,1)}, f32[2,512,512]{2,1,0:T(8,128)}, bf16[512,512]{1,0:T(8,128)(2,1)}, f32[8,512]{1,0:T(8,128)}, f32[2,512]{1,0:T(2,128)}) custom-call(bf16[128,2048]{1,0:T(8,128)(2,1)} %get-tuple-element.114.refs_0_, bf16[128,2048]{1,0:T(8,128)(2,1)} %collective-permute-done.29.refs_1_, ...), custom_call_target="tpu_custom_call" | custom-call | flops 174483046400 | bytes 1048576000 | tf_op jit(solution)/shard_map/attend_back/pallas_call | solution.py:125
  304.7 10.1 %project_back.1 = (bf16[3,512,512]{2,1,0:T(8,128)(2,1)}, f32[128,2048]{1,0:T(8,128)}, bf16[128,2048]{1,0:T(8,128)(2,1)}, bf16[128,2048]{1,0:T(8,128)(2,1)}, bf16[128,2048]{1,0:T(8,128)(2,1)}) custom-call(f32[2,512,512]{2,1,0:T(8,128)} %get-tuple-element.124.refs_0_, bf16[512,512]{1,0:T(8,128)(2,1)} %get-tuple-element.125.refs_1_, ...), custom_call_target="tpu_custom_call" | custom-call | flops 3221225 | bytes 14155 | tf_op jit(solution)/shard_map/project_back/pallas_call | solution.py:125
  324.9 8.1 %grad_rows_of.6 = (bf16[1024,1536]{1,0:T(8,128)(2,1)}, bf16[512,1536]{1,0:T(8,128)(2,1)}, bf16[256,1536]{1,0:T(8,128)(2,1)}, f32[256,1536]{1,0:T(8,128)}) custom-call(s32[8]{0:T(128)} %broadcast_xor_fusion.refs_0_, bf16[512,2048]{1,0:T(8,128)(2,1)} %get-tuple-element.133.refs_1_.refs_2_.refs_3_.refs_4_.refs_5_.refs_6_.refs_7_.refs_8_, ...), custom_call_target="tpu_custom_call" | custom-call | flops 3221225 | bytes 9961 | tf_op jit(solution)/shard_map/grad_rows_of/pallas_call | solution.py:125
  333.0 4.5 %grad_rows_of.7 = (bf16[1024,512]{1,0:T(8,128)(2,1)}, bf16[512,512]{1,0:T(8,128)(2,1)}, bf16[256,512]{1,0:T(8,128)(2,1)}, f32[256,512]{1,0:T(8,128)}) custom-call(s32[8]{0:T(128)} %broadcast_xor_fusion.refs_0_, bf16[512,2048]{1,0:T(8,128)(2,1)} %get-tuple-element.128.refs_2_.refs_1_.refs_3_.refs_4_.refs_5_.refs_6_.refs_7_.refs_8_, ...), custom_call_target="tpu_custom_call" | custom-call | flops 1073741 | bytes 4718 | tf_op jit(solution)/shard_map/grad_rows_of/pallas_call | solution.py:125
  357.6 5.8 %OwnersSum_finish.4.refs_3_ = f32[2,256,2048]{2,1,0:T(8,128)} custom-call(f32[256,4096]{1,0:T(8,128)} %get-tuple-element.143.refs_0_, bf16[512,4096]{1,0:T(8,128)(2,1)} %collective-permute-done.32.refs_1_.refs_3_, bf16[256,2048]{1,0:T(8,128)(2,1)} %collective-permute-done.37.refs_11_.refs_2_, bf16[512,4096]{1,0:T(8,128)(2,1)} %collective-permute-done.32.refs_1_.refs_3_, ...), custom_call_target="tpu_custom_call" | custom-call | flops 4194 | bytes 12582 | tf_op jit(solution)/shard_map/OwnersSum_finish/pallas_call | solution.py:125
  370.6 8.4 %collective-permute-done.51.refs_2_.refs_5_ = bf16[512,512]{1,0:T(8,128)(2,1)S(1)} collective-permute-done((bf16[512,512]{1,0:T(8,128)(2,1)}, bf16[512,512]{1,0:T(8,128)(2,1)S(1)}, u32[]{:S(2)}, u32[]{:S(2)}) %collective-permute-start.51) | collective-permute-done | bytes 524320 | tf_op jit(solution)/shard_map/ppermute | solution.py:19
  381.7 14.1 %collective-permute-done.53.refs_2_.refs_8_ = bf16[512,512]{1,0:T(8,128)(2,1)S(1)} collective-permute-done((bf16[512,512]{1,0:T(8,128)(2,1)}, bf16[512,512]{1,0:T(8,128)(2,1)S(1)}, u32[]{:S(2)}, u32[]{:S(2)}) %collective-permute-start.53) | collective-permute-done | bytes 524320 | tf_op jit(solution)/shard_map/ppermute | solution.py:19
  416.8 11.1 %collective-permute-done.54.refs_9_ = bf16[256,512]{1,0:T(8,128)(2,1)S(1)} collective-permute-done((bf16[256,512]{1,0:T(8,128)(2,1)S(1)}, bf16[256,512]{1,0:T(8,128)(2,1)S(1)}, u32[]{:S(2)}, u32[]{:S(2)}) %collective-permute-start.54) | collective-permute-done | bytes 262176 | tf_op jit(solution)/shard_map/ppermute | solution.py:19
  (261 shorter events, 166.0 us)
Async XLA Ops:
  3.7 24.8 %collective-permute-start = (bf16[128,2048]{1,0:T(8,128)(2,1)}, bf16[128,2048]{1,0:T(8,128)(2,1)S(1)}, u32[]{:S(2)}, u32[]{:S(2)}) collective-permute-start(bf16[128,2048]{1,0:T(8,128)(2,1)} %bitcast.47), channel_id=1, source_target_pairs={{0,2},{1,3},{2,0},{3,1},{4,6},{5,7},{6,4},{7,5},{8,10},{9,11},{10,... | collective-permute-start | bytes 1572872 | tf_op jit(solution)/shard_map/ppermute | solution.py:19
  103.5 25.3 %collective-permute-start.13 = (bf16[128,2048]{1,0:T(8,128)(2,1)S(1)}, bf16[128,2048]{1,0:T(8,128)(2,1)S(1)}, u32[]{:S(2)}, u32[]{:S(2)}) collective-permute-start(bf16[128,2048]{1,0:T(8,128)(2,1)S(1)} %collective-permute-done.12.refs_0_), channel_id=1, source_target_pairs={{0,1},{1,0},{2,3},{3,2},{4,5},{5,4},{6,7},{7,6},{8,9},{9,8},{10,11... | collective-permute-start | bytes 1572872 | tf_op jit(solution)/shard_map/ppermute | solution.py:19
  103.5 25.4 %collective-permute-start.14 = (bf16[128,2048]{1,0:T(8,128)(2,1)S(1)}, bf16[128,2048]{1,0:T(8,128)(2,1)S(1)}, u32[]{:S(2)}, u32[]{:S(2)}) collective-permute-start(bf16[128,2048]{1,0:T(8,128)(2,1)S(1)} %collective-permute-done.12.refs_0_), channel_id=1, source_target_pairs={{0,2},{1,3},{2,0},{3,1},{4,6},{5,7},{6,4},{7,5},{8,10},{9,11},{10,... | collective-permute-start | bytes 1572872 | tf_op jit(solution)/shard_map/ppermute | solution.py:19
  104.9 24.0 %collective-permute-start.15 = (bf16[128,2048]{1,0:T(8,128)(2,1)S(1)}, bf16[128,2048]{1,0:T(8,128)(2,1)S(1)}, u32[]{:S(2)}, u32[]{:S(2)}) collective-permute-start(bf16[128,2048]{1,0:T(8,128)(2,1)S(1)} %collective-permute-done.12.refs_0_), channel_id=1, source_target_pairs={{0,3},{1,2},{2,1},{3,0},{4,7},{5,6},{6,5},{7,4},{8,11},{9,10},{10,... | collective-permute-start | bytes 1572872 | tf_op jit(solution)/shard_map/ppermute | solution.py:19
  160.0 24.4 %collective-permute-start.25 = (bf16[128,2048]{1,0:T(8,128)(2,1)}, bf16[128,2048]{1,0:T(8,128)(2,1)S(1)}, u32[]{:S(2)}, u32[]{:S(2)}) collective-permute-start(bf16[128,2048]{1,0:T(8,128)(2,1)} %get-tuple-element.103.refs_0_), channel_id=1, source_target_pairs={{0,16},{4,20},{8,24},{12,28},{16,0},{20,4},{24,8},{28,12},{1,17},{... | collective-permute-start | bytes 1572872 | tf_op jit(solution)/shard_map/ppermute | solution.py:19
  160.0 24.7 %collective-permute-start.19 = (bf16[128,2048]{1,0:T(8,128)(2,1)}, bf16[128,2048]{1,0:T(8,128)(2,1)S(1)}, u32[]{:S(2)}, u32[]{:S(2)}) collective-permute-start(bf16[128,2048]{1,0:T(8,128)(2,1)} %get-tuple-element.103.refs_0_), channel_id=1, source_target_pairs={{0,1},{1,0},{2,3},{3,2},{4,5},{5,4},{6,7},{7,6},{8,9},{9,8},{10,11... | collective-permute-start | bytes 1572872 | tf_op jit(solution)/shard_map/ppermute | solution.py:19
  160.9 27.6 %collective-permute-start.20 = (bf16[128,2048]{1,0:T(8,128)(2,1)}, bf16[128,2048]{1,0:T(8,128)(2,1)S(1)}, u32[]{:S(2)}, u32[]{:S(2)}) collective-permute-start(bf16[128,2048]{1,0:T(8,128)(2,1)} %get-tuple-element.103.refs_0_), channel_id=1, source_target_pairs={{0,2},{1,3},{2,0},{3,1},{4,6},{5,7},{6,4},{7,5},{8,10},{9,11},{10,... | collective-permute-start | bytes 1572872 | tf_op jit(solution)/shard_map/ppermute | solution.py:19
  162.6 25.8 %collective-permute-start.21 = (bf16[128,2048]{1,0:T(8,128)(2,1)}, bf16[128,2048]{1,0:T(8,128)(2,1)}, u32[]{:S(2)}, u32[]{:S(2)}) collective-permute-start(bf16[128,2048]{1,0:T(8,128)(2,1)} %get-tuple-element.103.refs_0_), channel_id=1, source_target_pairs={{0,3},{1,2},{2,1},{3,0},{4,7},{5,6},{6,5},{7,4},{8,11},{9,10},{10,... | collective-permute-start | bytes 1572872 | tf_op jit(solution)/shard_map/ppermute | solution.py:19
  184.4 28.0 %collective-permute-start.26 = (bf16[128,2048]{1,0:T(8,128)(2,1)S(1)}, bf16[128,2048]{1,0:T(8,128)(2,1)S(1)}, u32[]{:S(2)}, u32[]{:S(2)}) collective-permute-start(bf16[128,2048]{1,0:T(8,128)(2,1)S(1)} %collective-permute-done.25.refs_4_), channel_id=1, source_target_pairs={{0,1},{1,0},{2,3},{3,2},{4,5},{5,4},{6,7},{7,6},{8,9},{9,8},{10,11... | collective-permute-start | bytes 1572872 | tf_op jit(solution)/shard_map/ppermute | solution.py:19
  184.8 30.5 %collective-permute-start.27 = (bf16[128,2048]{1,0:T(8,128)(2,1)S(1)}, bf16[128,2048]{1,0:T(8,128)(2,1)S(1)}, u32[]{:S(2)}, u32[]{:S(2)}) collective-permute-start(bf16[128,2048]{1,0:T(8,128)(2,1)S(1)} %collective-permute-done.25.refs_4_), channel_id=1, source_target_pairs={{0,2},{1,3},{2,0},{3,1},{4,6},{5,7},{6,4},{7,5},{8,10},{9,11},{10,... | collective-permute-start | bytes 1572872 | tf_op jit(solution)/shard_map/ppermute | solution.py:19
  184.8 30.5 %collective-permute-start.28 = (bf16[128,2048]{1,0:T(8,128)(2,1)S(1)}, bf16[128,2048]{1,0:T(8,128)(2,1)S(1)}, u32[]{:S(2)}, u32[]{:S(2)}) collective-permute-start(bf16[128,2048]{1,0:T(8,128)(2,1)S(1)} %collective-permute-done.25.refs_4_), channel_id=1, source_target_pairs={{0,3},{1,2},{2,1},{3,0},{4,7},{5,6},{6,5},{7,4},{8,11},{9,10},{10,... | collective-permute-start | bytes 1572872 | tf_op jit(solution)/shard_map/ppermute | solution.py:19
  211.7 40.4 %collective-permute-start.22 = (bf16[128,2048]{1,0:T(8,128)(2,1)}, bf16[128,2048]{1,0:T(8,128)(2,1)}, u32[]{:S(2)}, u32[]{:S(2)}) collective-permute-start(bf16[128,2048]{1,0:T(8,128)(2,1)} %get-tuple-element.105), channel_id=1, source_target_pairs={{0,1},{1,0},{2,3},{3,2},{4,5},{5,4},{6,7},{7,6},{8,9},{9,8},{10,11... | collective-permute-start | bytes 1572872 | tf_op jit(solution)/shard_map/ppermute | solution.py:19
  212.1 40.0 %collective-permute-start.23 = (bf16[128,2048]{1,0:T(8,128)(2,1)}, bf16[128,2048]{1,0:T(8,128)(2,1)}, u32[]{:S(2)}, u32[]{:S(2)}) collective-permute-start(bf16[128,2048]{1,0:T(8,128)(2,1)} %get-tuple-element.106), channel_id=1, source_target_pairs={{0,2},{1,3},{2,0},{3,1},{4,6},{5,7},{6,4},{7,5},{8,10},{9,11},{10,... | collective-permute-start | bytes 1572872 | tf_op jit(solution)/shard_map/ppermute | solution.py:19
  212.4 39.7 %collective-permute-start.24 = (bf16[128,2048]{1,0:T(8,128)(2,1)}, bf16[128,2048]{1,0:T(8,128)(2,1)}, u32[]{:S(2)}, u32[]{:S(2)}) collective-permute-start(bf16[128,2048]{1,0:T(8,128)(2,1)} %get-tuple-element.107), channel_id=1, source_target_pairs={{0,3},{1,2},{2,1},{3,0},{4,7},{5,6},{6,5},{7,4},{8,11},{9,10},{10,... | collective-permute-start | bytes 1572872 | tf_op jit(solution)/shard_map/ppermute | solution.py:19
  257.1 25.6 %collective-permute-start.30 = (bf16[128,2048]{1,0:T(8,128)(2,1)}, bf16[128,2048]{1,0:T(8,128)(2,1)}, u32[]{:S(2)}, u32[]{:S(2)}) collective-permute-start(bf16[128,2048]{1,0:T(8,128)(2,1)} %get-tuple-element.114.refs_0_), channel_id=1, source_target_pairs={{0,2},{1,3},{2,0},{3,1},{4,6},{5,7},{6,4},{7,5},{8,10},{9,11},{10,... | collective-permute-start | bytes 1572872 | tf_op jit(solution)/shard_map/ppermute | solution.py:19
  257.4 25.2 %collective-permute-start.31 = (bf16[128,2048]{1,0:T(8,128)(2,1)}, bf16[128,2048]{1,0:T(8,128)(2,1)}, u32[]{:S(2)}, u32[]{:S(2)}) collective-permute-start(bf16[128,2048]{1,0:T(8,128)(2,1)} %get-tuple-element.114.refs_0_), channel_id=1, source_target_pairs={{0,3},{1,2},{2,1},{3,0},{4,7},{5,6},{6,5},{7,4},{8,11},{9,10},{10,... | collective-permute-start | bytes 1572872 | tf_op jit(solution)/shard_map/ppermute | solution.py:19
  262.9 41.1 %collective-permute-start.37 = (bf16[256,2048]{1,0:T(8,128)(2,1)}, bf16[256,2048]{1,0:T(8,128)(2,1)}, u32[]{:S(2)}, u32[]{:S(2)}) collective-permute-start(bf16[256,2048]{1,0:T(8,128)(2,1)} %add_parts.11.refs_11_), channel_id=1, source_target_pairs={{0,8},{4,12},{8,0},{12,4},{16,24},{20,28},{24,16},{28,20},{1,9},{5... | collective-permute-start | bytes 3145736 | tf_op jit(solution)/shard_map/ppermute | solution.py:19
  277.2 47.1 %collective-permute-start.41 = (bf16[256,2048]{1,0:T(8,128)(2,1)}, bf16[256,2048]{1,0:T(8,128)(2,1)}, u32[]{:S(2)}, u32[]{:S(2)}) collective-permute-start(bf16[256,2048]{1,0:T(8,128)(2,1)} %add_parts.12.refs_14_), channel_id=1, source_target_pairs={{0,8},{4,12},{8,0},{12,4},{16,24},{20,28},{24,16},{28,20},{1,9},{5... | collective-permute-start | bytes 3145736 | tf_op jit(solution)/shard_map/ppermute | solution.py:19
  300.6 41.9 %collective-permute-start.43 = (bf16[256,2048]{1,0:T(8,128)(2,1)}, bf16[256,2048]{1,0:T(8,128)(2,1)S(1)}, u32[]{:S(2)}, u32[]{:S(2)}) collective-permute-start(bf16[256,2048]{1,0:T(8,128)(2,1)} %add_parts.13.refs_10_), channel_id=1, source_target_pairs={{0,8},{4,12},{8,0},{12,4},{16,24},{20,28},{24,16},{28,20},{1,9},{5... | collective-permute-start | bytes 3145736 | tf_op jit(solution)/shard_map/ppermute | solution.py:19
  349.6 29.4 %collective-permute-start.51 = (bf16[512,512]{1,0:T(8,128)(2,1)}, bf16[512,512]{1,0:T(8,128)(2,1)S(1)}, u32[]{:S(2)}, u32[]{:S(2)}) collective-permute-start(bf16[512,512]{1,0:T(8,128)(2,1)} %add_parts.15.refs_2_), channel_id=1, source_target_pairs={{0,8},{4,12},{8,0},{12,4},{16,24},{20,28},{24,16},{28,20},{1,9},{5... | collective-permute-start | bytes 1572872 | tf_op jit(solution)/shard_map/ppermute | solution.py:19
  353.5 42.4 %collective-permute-start.53 = (bf16[512,512]{1,0:T(8,128)(2,1)}, bf16[512,512]{1,0:T(8,128)(2,1)S(1)}, u32[]{:S(2)}, u32[]{:S(2)}) collective-permute-start(bf16[512,512]{1,0:T(8,128)(2,1)} %add_parts.16.refs_2_), channel_id=1, source_target_pairs={{0,8},{4,12},{8,0},{12,4},{16,24},{20,28},{24,16},{28,20},{1,9},{5... | collective-permute-start | bytes 1572872 | tf_op jit(solution)/shard_map/ppermute | solution.py:19
  355.8 49.3 %collective-permute-start.55 = (bf16[512,512]{1,0:T(8,128)(2,1)}, bf16[512,512]{1,0:T(8,128)(2,1)S(1)}, u32[]{:S(2)}, u32[]{:S(2)}) collective-permute-start(bf16[512,512]{1,0:T(8,128)(2,1)} %add_parts.17.refs_5_), channel_id=1, source_target_pairs={{0,8},{4,12},{8,0},{12,4},{16,24},{20,28},{24,16},{28,20},{1,9},{5... | collective-permute-start | bytes 1572872 | tf_op jit(solution)/shard_map/ppermute | solution.py:19
  366.1 33.2 %collective-permute-start.50 = (bf16[256,512]{1,0:T(8,128)(2,1)}, bf16[256,512]{1,0:T(8,128)(2,1)S(1)}, u32[]{:S(2)}, u32[]{:S(2)}) collective-permute-start(bf16[256,512]{1,0:T(8,128)(2,1)} %add_parts.18.refs_3_), channel_id=1, source_target_pairs={{0,16},{4,20},{8,24},{12,28},{16,0},{20,4},{24,8},{28,12},{1,17},{... | collective-permute-start | bytes 786440 | tf_op jit(solution)/shard_map/ppermute | solution.py:19
  409.0 23.8 %collective-permute-start.57 = (bf16[256,512]{1,0:T(8,128)(2,1)}, bf16[256,512]{1,0:T(8,128)(2,1)S(1)}, u32[]{:S(2)}, u32[]{:S(2)}) collective-permute-start(bf16[256,512]{1,0:T(8,128)(2,1)} %add_parts.21.refs_1_), channel_id=1, source_target_pairs={{0,16},{4,20},{8,24},{12,28},{16,0},{20,4},{24,8},{28,12},{1,17},{... | collective-permute-start | bytes 786440 | tf_op jit(solution)/shard_map/ppermute | solution.py:19
  (83 other events, 760.1 us)

commit v2 on v1

--- a/solution.py
+++ b/solution.py
@@ -1068,9 +1068,15 @@
     order.append(gate_up_sum.latest(1))
     qkv_sum = OwnersSum(order, [(x_full, d_projected, 0, rows)], replicas, 3)
     out_sum = OwnersSum(order, [(d_attn_full, context[None], 0, rows)], replicas)
-    fence(order, [down_sum.latest(), *input_parts[1:], gains])
+    fence(order, [down_sum.latest(), gains])
     qkv_sum.step(order)
     out_sum.step(order)
+    order.extend(input_parts[1:])
+    [gains] = gate(order, [gains])
+    flip = 2
+    while flip < far:
+        gains = gains + exchange(gains, "replica", flip)
+        flip *= 2
     gate_up_grad = gate_up_sum.finish(order, 2, False)
     qkv_sum.at += 1
     qkv_sum.send(order, 0)
@@ -1079,13 +1085,8 @@
     order.append(qkv_sum.latest(0))
     qkv_sum.send(order, 2)
     order.append(qkv_sum.latest(1))
+    order.append(gains)
     out_sum.step(order)
-    [gains] = gate(order, [gains])
-    flip = 2
-    while flip < far:
-        gains = gains + exchange(gains, "replica", flip)
-        flip *= 2
-    order.append(gains)
     qkv_grad = qkv_sum.finish(order, 3, False)
     out_grad = out_sum.finish(order, 1, True)
     [far_gains] = gate(order, [exchange(gains, "replica", far)])

time: 439 us -> 437 us (level)
    unnamed x96 -> x94, local copies, waits for them, and re-layouts: 15.2 us -> 14 us
  transfers between devices with their start and end apart: 59 -> 59, of which waited for: 24 -> 23; matrix products, arithmetic and copies ran while one was open for 3% -> 3% of each run, Pallas kernels for 40% -> 41%
where the time goes in v2:
time: 437 us; the launch traced here: 435 us
  Pallas kernels  201 us (46%)
  waiting for transfers between devices  141 us (32%)
  starting transfers between devices  63.8 us (15%)
  local copies, waits for them, and re-layouts  15.5 us (4%)
  other arithmetic  10.2 us (2%)
    pallas_call x36, Pallas kernels, launch(): results = pl.pallas_call(body, **settings)(*args, *waits)  201 us
    ppermute x59, waiting for transfers between devices, exchange(): return lax.ppermute(value, axis, [(i, i ^ flip) for i in range(size)])  141 us
    ppermute x59, starting transfers between devices, exchange(): return lax.ppermute(value, axis, [(i, i ^ flip) for i in range(size)])  63.8 us
    unnamed x94, local copies, waits for them, and re-layouts  14 us
  transfers between devices with their start and end apart: 59, of which 23 were waited for; matrix products, arithmetic and copies ran while one was open for 3% of the time, Pallas kernels for 41%

profile of v2, /device:TPU:0, one launch (start us, length us, event | category | flops | bytes accessed | tf_op | source)
XLA Modules:
  0.0 435.0 jit_solution(6495385106558993281)
XLA Ops:
  10.9 5.7 %collective-permute-done.2.refs_1_ = bf16[128,2048]{1,0:T(8,128)(2,1)S(1)} collective-permute-done((bf16[128,2048]{1,0:T(8,128)(2,1)}, bf16[128,2048]{1,0:T(8,128)(2,1)S(1)}, u32[]{:S(2)}, u32[]{:S(2)}) %collective-permute-start.2) | collective-permute-done | bytes 524320 | tf_op jit(solution)/shard_map/ppermute | solution.py:19
  17.4 7.0 %project.2 = (f32[2,512,512]{2,1,0:T(8,128)}, bf16[512,512]{1,0:T(8,128)(2,1)}, f32[8,512]{1,0:T(8,128)}, bf16[512,2048]{1,0:T(8,128)(2,1)}) custom-call(bf16[128,2048]{1,0:T(8,128)(2,1)} %bitcast.49, bf16[128,2048]{1,0:T(8,128)(2,1)} %copy-done.21, bf16[3,2048,512]{2,1,0:T(8,128)(2,1)} %refs_5_.7), custom_call_target="tpu_custom_call" | custom-call | flops 1610612 | bytes 7340 | tf_op jit(solution)/shard_map/project/pallas_call | solution.py:125
  29.5 6.9 %project.3 = (f32[2,512,512]{2,1,0:T(8,128)}, bf16[512,512]{1,0:T(8,128)(2,1)}, f32[8,512]{1,0:T(8,128)}, bf16[512,2048]{1,0:T(8,128)(2,1)}) custom-call(bf16[128,2048]{1,0:T(8,128)(2,1)} %copy-done.22, bf16[128,2048]{1,0:T(8,128)(2,1)} %copy-done.23, ...), custom_call_target="tpu_custom_call", output_to_operand_aliasing={{0}: (3, {}), {1}: (4, {}), {2}: (5, {}), {3}: (6, {})} | custom-call | flops 1610612 | bytes 7340 | tf_op jit(solution)/shard_map/project/pallas_call | solution.py:125
  43.9 8.8 %attend.1 = (bf16[512,512]{1,0:T(8,128)(2,1)}, bf16[512,512]{1,0:T(8,128)(2,1)}, bf16[512,512]{1,0:T(8,128)(2,1)}, f32[512,8]{1,0:T(8,128)}, f32[128,2048]{1,0:T...) custom-call(f32[2,512,512]{2,1,0:T(8,128)} %get-tuple-element.82.refs_0_.refs_11_.refs_2_, ...), custom_call_target="tpu_custom_call" | custom-call | flops 1342177 | bytes 7864 | tf_op jit(solution)/shard_map/attend/pallas_call | solution.py:125
  56.1 11.5 %collective-permute-done.6.refs_1_ = bf16[128,2048]{1,0:T(8,128)(2,1)S(1)} collective-permute-done((bf16[128,2048]{1,0:T(8,128)(2,1)}, bf16[128,2048]{1,0:T(8,128)(2,1)S(1)}, u32[]{:S(2)}, u32[]{:S(2)}) %collective-permute-start.6) | collective-permute-done | bytes 524320 | tf_op jit(solution)/shard_map/ppermute | solution.py:19
  67.7 6.5 %collective-permute-done.7.refs_2_ = bf16[128,2048]{1,0:T(8,128)(2,1)S(1)} collective-permute-done((bf16[128,2048]{1,0:T(8,128)(2,1)}, bf16[128,2048]{1,0:T(8,128)(2,1)S(1)}, u32[]{:S(2)}, u32[]{:S(2)}) %collective-permute-start.7) | collective-permute-done | bytes 524320 | tf_op jit(solution)/shard_map/ppermute | solution.py:19
  86.8 16.7 %collective-permute-done.12.refs_0_ = bf16[128,2048]{1,0:T(8,128)(2,1)S(1)} collective-permute-done((bf16[128,2048]{1,0:T(8,128)(2,1)}, bf16[128,2048]{1,0:T(8,128)(2,1)S(1)}, u32[]{:S(2)}, u32[]{:S(2)}) %collective-permute-start.12) | collective-permute-done | bytes 524320 | tf_op jit(solution)/shard_map/ppermute | solution.py:19
  107.8 21.0 %mlp_forward.1 = (bf16[2,512,2048]{2,1,0:T(8,128)(2,1)}, bf16[512,2048]{1,0:T(8,128)(2,1)}, bf16[512,2048]{1,0:T(8,128)(2,1)}, f32[128,2048]{1,0:T(8,128)}, bf16...) custom-call(bf16[128,2048]{1,0:T(8,128)(2,1)} %get-tuple-element.90.refs_0_, ...), custom_call_target="tpu_custom_call" | custom-call | flops 12884901 | bytes 39845 | tf_op jit(solution)/shard_map/mlp_forward/pallas_call | solution.py:125
  133.5 11.5 %collective-permute-done.16.refs_1_ = bf16[128,2048]{1,0:T(8,128)(2,1)S(1)} collective-permute-done((bf16[128,2048]{1,0:T(8,128)(2,1)}, bf16[128,2048]{1,0:T(8,128)(2,1)S(1)}, u32[]{:S(2)}, u32[]{:S(2)}) %collective-permute-start.16) | collective-permute-done | bytes 524320 | tf_op jit(solution)/shard_map/ppermute | solution.py:19
  145.0 8.0 %collective-permute-done.17.refs_2_ = bf16[128,2048]{1,0:T(8,128)(2,1)S(1)} collective-permute-done((bf16[128,2048]{1,0:T(8,128)(2,1)}, bf16[128,2048]{1,0:T(8,128)(2,1)S(1)}, u32[]{:S(2)}, u32[]{:S(2)}) %collective-permute-start.17) | collective-permute-done | bytes 524320 | tf_op jit(solution)/shard_map/ppermute | solution.py:19
  155.4 4.5 %after_mlp.1 = (f32[128,2048]{1,0:T(8,128)}, bf16[128,2048]{1,0:T(8,128)(2,1)}, f32[1,2048]{1,0:T(1,128)}) custom-call(f32[128,2048]{1,0:T(8,128)} %get-tuple-element.97.refs_0_.refs_7_, bf16[128,2048]{1,0:T(8,128)(2,1)} %copy-done.24, bf16[128,2048]{1,0:T(8,128)(2,1)} %copy-done.26, bf16[128,2048]{1,0:T(8,128)(2,1)} %copy-done.28, ...), custom_call_target="tpu_custom_call" | custom-call | flops 4194 | bytes 6291 | tf_op jit(solution)/shard_map/after_mlp/pallas_call | solution.py:125
  163.6 20.8 %collective-permute-done.25.refs_4_ = bf16[128,2048]{1,0:T(8,128)(2,1)S(1)} collective-permute-done((bf16[128,2048]{1,0:T(8,128)(2,1)}, bf16[128,2048]{1,0:T(8,128)(2,1)S(1)}, u32[]{:S(2)}, u32[]{:S(2)}) %collective-permute-start.25) | collective-permute-done | bytes 524320 | tf_op jit(solution)/shard_map/ppermute | solution.py:19
  189.2 22.5 %mlp_back.1 = (bf16[2,512,2048]{2,1,0:T(8,128)(2,1)}, bf16[512,2048]{1,0:T(8,128)(2,1)}, f32[128,2048]{1,0:T(8,128)}, bf16[128,2048]{1,0:T(8,128)(2,1)}, bf16[12...) custom-call(bf16[128,2048]{1,0:T(8,128)(2,1)} %get-tuple-element.103.refs_0_, bf16[128,2048]{1,0:T(8,128)(2,1)} %copy-done.17, ...), custom_call_target="tpu_custom_call" | custom-call | flops 12884901 | bytes 41943 | tf_op jit(solution)/shard_map/mlp_back/pallas_call | solution.py:125
  216.8 20.6 %mlp_units.1 = (bf16[2,512,2048]{2,1,0:T(8,128)(2,1)}, bf16[512,2048]{1,0:T(8,128)(2,1)}, bf16[512,2048]{1,0:T(8,128)(2,1)}, bf16[512,2048]{1,0:T(8,128)(2,1)}) custom-call(bf16[128,2048]{1,0:T(8,128)(2,1)} %copy-done.12, bf16[128,2048]{1,0:T(8,128)(2,1)} %copy-done.1, bf16[128,2048]{1,0:T(8,128)(2,1)} %copy-done.2, bf16[128,2048]{1,0:T(8,128)(2,1)} %copy-done.3, ...), custom_call_target="tpu_custom_call" | custom-call | flops 12884901 | bytes 37748 | tf_op jit(solution)/shard_map/mlp_units/pallas_call | solution.py:125
  237.4 14.7 %grad_rows_of.4 = (bf16[512,4096]{1,0:T(8,128)(2,1)}, bf16[256,4096]{1,0:T(8,128)(2,1)}, f32[256,4096]{1,0:T(8,128)}) custom-call(s32[4]{0:T(128)} %broadcast_xor_fusion.1.refs_0_, bf16[512,2048]{1,0:T(8,128)(2,1)} %get-tuple-element.108.refs_1_.refs_2_.refs_3_.refs_4_, bf16[512,2048]{1,0:T(8,128)(2,1)} %get-tuple-element.108.refs_1_.refs_2_.refs_3_.refs_4_, ...), custom_call_target="tpu_custom_call" | custom-call | flops 8589934 | bytes 18874 | tf_op jit(solution)/shard_map/grad_rows_of/pallas_call | solution.py:125
  265.0 9.3 %grad_rows_of.5 = (bf16[512,2048]{1,0:T(8,128)(2,1)}, bf16[256,2048]{1,0:T(8,128)(2,1)}, f32[256,2048]{1,0:T(8,128)}) custom-call(s32[4]{0:T(128)} %broadcast_xor_fusion.1.refs_0_, bf16[512,2048]{1,0:T(8,128)(2,1)} %get-tuple-element.119.refs_1_.refs_2_.refs_3_.refs_4_, bf16[512,2048]{1,0:T(8,128)(2,1)} %get-tuple-element.119.refs_1_.refs_2_.refs_3_.refs_4_, ...), custom_call_target="tpu_custom_call" | custom-call | flops 429496729600 | bytes 1048576000 | tf_op jit(solution)/shard_map/grad_rows_of/pallas_call | solution.py:125
  277.2 5.4 %collective-permute-done.30.refs_2_ = bf16[128,2048]{1,0:T(8,128)(2,1)} collective-permute-done((bf16[128,2048]{1,0:T(8,128)(2,1)}, bf16[128,2048]{1,0:T(8,128)(2,1)}, u32[]{:S(2)}, u32[]{:S(2)}) %collective-permute-start.30) | collective-permute-done | bytes 524320 | tf_op jit(solution)/shard_map/ppermute | solution.py:19
  282.6 11.7 %attend_back.1 = (bf16[512,2048]{1,0:T(8,128)(2,1)}, f32[2,512,512]{2,1,0:T(8,128)}, bf16[512,512]{1,0:T(8,128)(2,1)}, f32[8,512]{1,0:T(8,128)}, f32[2,512]{1,0:T(2,128)}) custom-call(bf16[128,2048]{1,0:T(8,128)(2,1)} %get-tuple-element.114.refs_0_, bf16[128,2048]{1,0:T(8,128)(2,1)} %collective-permute-done.29.refs_1_, ...), custom_call_target="tpu_custom_call" | custom-call | flops 174483046400 | bytes 1048576000 | tf_op jit(solution)/shard_map/attend_back/pallas_call | solution.py:125
  304.7 10.1 %project_back.1 = (bf16[3,512,512]{2,1,0:T(8,128)(2,1)}, f32[128,2048]{1,0:T(8,128)}, bf16[128,2048]{1,0:T(8,128)(2,1)}, bf16[128,2048]{1,0:T(8,128)(2,1)}, bf16[128,2048]{1,0:T(8,128)(2,1)}) custom-call(f32[2,512,512]{2,1,0:T(8,128)} %get-tuple-element.124.refs_0_, bf16[512,512]{1,0:T(8,128)(2,1)} %get-tuple-element.125.refs_1_, ...), custom_call_target="tpu_custom_call" | custom-call | flops 3221225 | bytes 14155 | tf_op jit(solution)/shard_map/project_back/pallas_call | solution.py:125
  323.1 8.1 %grad_rows_of.6 = (bf16[1024,1536]{1,0:T(8,128)(2,1)}, bf16[512,1536]{1,0:T(8,128)(2,1)}, bf16[256,1536]{1,0:T(8,128)(2,1)}, f32[256,1536]{1,0:T(8,128)}) custom-call(s32[8]{0:T(128)} %broadcast_xor_fusion.refs_0_, bf16[512,2048]{1,0:T(8,128)(2,1)} %get-tuple-element.133.refs_1_.refs_2_.refs_3_.refs_4_.refs_5_.refs_6_.refs_7_.refs_8_, ...), custom_call_target="tpu_custom_call" | custom-call | flops 3221225 | bytes 9961 | tf_op jit(solution)/shard_map/grad_rows_of/pallas_call | solution.py:125
  345.4 6.0 %collective-permute-done.38.refs_2_ = bf16[128,2048]{1,0:T(8,128)(2,1)} collective-permute-done((bf16[128,2048]{1,0:T(8,128)(2,1)}, bf16[128,2048]{1,0:T(8,128)(2,1)}, u32[]{:S(2)}, u32[]{:S(2)}) %collective-permute-start.38) | collective-permute-done | bytes 524320 | tf_op jit(solution)/shard_map/ppermute | solution.py:19
  363.0 5.8 %OwnersSum_finish.4.refs_3_ = f32[2,256,2048]{2,1,0:T(8,128)} custom-call(f32[256,4096]{1,0:T(8,128)} %get-tuple-element.143.refs_0_, bf16[512,4096]{1,0:T(8,128)(2,1)} %collective-permute-done.32.refs_1_.refs_3_, bf16[256,2048]{1,0:T(8,128)(2,1)} %collective-permute-done.37.refs_11_.refs_2_, bf16[512,4096]{1,0:T(8,128)(2,1)} %collective-permute-done.32.refs_1_.refs_3_, ...), custom_call_target="tpu_custom_call" | custom-call | flops 4194 | bytes 12582 | tf_op jit(solution)/shard_map/OwnersSum_finish/pallas_call | solution.py:125
  382.3 19.7 %collective-permute-done.56 = f32[4,512]{1,0:T(4,128)S(1)} collective-permute-done((f32[4,512]{1,0:T(4,128)S(1)}, f32[4,512]{1,0:T(4,128)S(1)}, u32[]{:S(2)}, u32[]{:S(2)}) %collective-permute-start.56) | collective-permute-done | bytes 8224 | tf_op jit(solution)/shard_map/ppermute | solution.py:19
  413.8 10.7 %collective-permute-done.54.refs_9_ = bf16[256,512]{1,0:T(8,128)(2,1)S(1)} collective-permute-done((bf16[256,512]{1,0:T(8,128)(2,1)}, bf16[256,512]{1,0:T(8,128)(2,1)S(1)}, u32[]{:S(2)}, u32[]{:S(2)}) %collective-permute-start.54) | collective-permute-done | bytes 262176 | tf_op jit(solution)/shard_map/ppermute | solution.py:19
  (259 shorter events, 160.5 us)
Async XLA Ops:
  3.7 24.8 %collective-permute-start = (bf16[128,2048]{1,0:T(8,128)(2,1)}, bf16[128,2048]{1,0:T(8,128)(2,1)S(1)}, u32[]{:S(2)}, u32[]{:S(2)}) collective-permute-start(bf16[128,2048]{1,0:T(8,128)(2,1)} %bitcast.47), channel_id=1, source_target_pairs={{0,2},{1,3},{2,0},{3,1},{4,6},{5,7},{6,4},{7,5},{8,10},{9,11},{10,... | collective-permute-start | bytes 1572872 | tf_op jit(solution)/shard_map/ppermute | solution.py:19
  103.5 25.3 %collective-permute-start.13 = (bf16[128,2048]{1,0:T(8,128)(2,1)S(1)}, bf16[128,2048]{1,0:T(8,128)(2,1)S(1)}, u32[]{:S(2)}, u32[]{:S(2)}) collective-permute-start(bf16[128,2048]{1,0:T(8,128)(2,1)S(1)} %collective-permute-done.12.refs_0_), channel_id=1, source_target_pairs={{0,1},{1,0},{2,3},{3,2},{4,5},{5,4},{6,7},{7,6},{8,9},{9,8},{10,11... | collective-permute-start | bytes 1572872 | tf_op jit(solution)/shard_map/ppermute | solution.py:19
  103.5 25.4 %collective-permute-start.14 = (bf16[128,2048]{1,0:T(8,128)(2,1)S(1)}, bf16[128,2048]{1,0:T(8,128)(2,1)S(1)}, u32[]{:S(2)}, u32[]{:S(2)}) collective-permute-start(bf16[128,2048]{1,0:T(8,128)(2,1)S(1)} %collective-permute-done.12.refs_0_), channel_id=1, source_target_pairs={{0,2},{1,3},{2,0},{3,1},{4,6},{5,7},{6,4},{7,5},{8,10},{9,11},{10,... | collective-permute-start | bytes 1572872 | tf_op jit(solution)/shard_map/ppermute | solution.py:19
  160.0 24.8 %collective-permute-start.19 = (bf16[128,2048]{1,0:T(8,128)(2,1)}, bf16[128,2048]{1,0:T(8,128)(2,1)S(1)}, u32[]{:S(2)}, u32[]{:S(2)}) collective-permute-start(bf16[128,2048]{1,0:T(8,128)(2,1)} %get-tuple-element.103.refs_0_), channel_id=1, source_target_pairs={{0,1},{1,0},{2,3},{3,2},{4,5},{5,4},{6,7},{7,6},{8,9},{9,8},{10,11... | collective-permute-start | bytes 1572872 | tf_op jit(solution)/shard_map/ppermute | solution.py:19
  160.8 27.5 %collective-permute-start.20 = (bf16[128,2048]{1,0:T(8,128)(2,1)}, bf16[128,2048]{1,0:T(8,128)(2,1)S(1)}, u32[]{:S(2)}, u32[]{:S(2)}) collective-permute-start(bf16[128,2048]{1,0:T(8,128)(2,1)} %get-tuple-element.103.refs_0_), channel_id=1, source_target_pairs={{0,2},{1,3},{2,0},{3,1},{4,6},{5,7},{6,4},{7,5},{8,10},{9,11},{10,... | collective-permute-start | bytes 1572872 | tf_op jit(solution)/shard_map/ppermute | solution.py:19
  162.6 25.8 %collective-permute-start.21 = (bf16[128,2048]{1,0:T(8,128)(2,1)}, bf16[128,2048]{1,0:T(8,128)(2,1)}, u32[]{:S(2)}, u32[]{:S(2)}) collective-permute-start(bf16[128,2048]{1,0:T(8,128)(2,1)} %get-tuple-element.103.refs_0_), channel_id=1, source_target_pairs={{0,3},{1,2},{2,1},{3,0},{4,7},{5,6},{6,5},{7,4},{8,11},{9,10},{10,... | collective-permute-start | bytes 1572872 | tf_op jit(solution)/shard_map/ppermute | solution.py:19
  184.4 28.0 %collective-permute-start.26 = (bf16[128,2048]{1,0:T(8,128)(2,1)S(1)}, bf16[128,2048]{1,0:T(8,128)(2,1)S(1)}, u32[]{:S(2)}, u32[]{:S(2)}) collective-permute-start(bf16[128,2048]{1,0:T(8,128)(2,1)S(1)} %collective-permute-done.25.refs_4_), channel_id=1, source_target_pairs={{0,1},{1,0},{2,3},{3,2},{4,5},{5,4},{6,7},{7,6},{8,9},{9,8},{10,11... | collective-permute-start | bytes 1572872 | tf_op jit(solution)/shard_map/ppermute | solution.py:19
  184.8 30.5 %collective-permute-start.27 = (bf16[128,2048]{1,0:T(8,128)(2,1)S(1)}, bf16[128,2048]{1,0:T(8,128)(2,1)S(1)}, u32[]{:S(2)}, u32[]{:S(2)}) collective-permute-start(bf16[128,2048]{1,0:T(8,128)(2,1)S(1)} %collective-permute-done.25.refs_4_), channel_id=1, source_target_pairs={{0,2},{1,3},{2,0},{3,1},{4,6},{5,7},{6,4},{7,5},{8,10},{9,11},{10,... | collective-permute-start | bytes 1572872 | tf_op jit(solution)/shard_map/ppermute | solution.py:19
  184.8 30.4 %collective-permute-start.28 = (bf16[128,2048]{1,0:T(8,128)(2,1)S(1)}, bf16[128,2048]{1,0:T(8,128)(2,1)S(1)}, u32[]{:S(2)}, u32[]{:S(2)}) collective-permute-start(bf16[128,2048]{1,0:T(8,128)(2,1)S(1)} %collective-permute-done.25.refs_4_), channel_id=1, source_target_pairs={{0,3},{1,2},{2,1},{3,0},{4,7},{5,6},{6,5},{7,4},{8,11},{9,10},{10,... | collective-permute-start | bytes 1572872 | tf_op jit(solution)/shard_map/ppermute | solution.py:19
  211.6 40.4 %collective-permute-start.22 = (bf16[128,2048]{1,0:T(8,128)(2,1)}, bf16[128,2048]{1,0:T(8,128)(2,1)}, u32[]{:S(2)}, u32[]{:S(2)}) collective-permute-start(bf16[128,2048]{1,0:T(8,128)(2,1)} %get-tuple-element.105), channel_id=1, source_target_pairs={{0,1},{1,0},{2,3},{3,2},{4,5},{5,4},{6,7},{7,6},{8,9},{9,8},{10,11... | collective-permute-start | bytes 1572872 | tf_op jit(solution)/shard_map/ppermute | solution.py:19
  212.1 39.9 %collective-permute-start.23 = (bf16[128,2048]{1,0:T(8,128)(2,1)}, bf16[128,2048]{1,0:T(8,128)(2,1)}, u32[]{:S(2)}, u32[]{:S(2)}) collective-permute-start(bf16[128,2048]{1,0:T(8,128)(2,1)} %get-tuple-element.106), channel_id=1, source_target_pairs={{0,2},{1,3},{2,0},{3,1},{4,6},{5,7},{6,4},{7,5},{8,10},{9,11},{10,... | collective-permute-start | bytes 1572872 | tf_op jit(solution)/shard_map/ppermute | solution.py:19
  212.4 39.7 %collective-permute-start.24 = (bf16[128,2048]{1,0:T(8,128)(2,1)}, bf16[128,2048]{1,0:T(8,128)(2,1)}, u32[]{:S(2)}, u32[]{:S(2)}) collective-permute-start(bf16[128,2048]{1,0:T(8,128)(2,1)} %get-tuple-element.107), channel_id=1, source_target_pairs={{0,3},{1,2},{2,1},{3,0},{4,7},{5,6},{6,5},{7,4},{8,11},{9,10},{10,... | collective-permute-start | bytes 1572872 | tf_op jit(solution)/shard_map/ppermute | solution.py:19
  257.0 25.6 %collective-permute-start.30 = (bf16[128,2048]{1,0:T(8,128)(2,1)}, bf16[128,2048]{1,0:T(8,128)(2,1)}, u32[]{:S(2)}, u32[]{:S(2)}) collective-permute-start(bf16[128,2048]{1,0:T(8,128)(2,1)} %get-tuple-element.114.refs_0_), channel_id=1, source_target_pairs={{0,2},{1,3},{2,0},{3,1},{4,6},{5,7},{6,4},{7,5},{8,10},{9,11},{10,... | collective-permute-start | bytes 1572872 | tf_op jit(solution)/shard_map/ppermute | solution.py:19
  257.3 25.2 %collective-permute-start.31 = (bf16[128,2048]{1,0:T(8,128)(2,1)}, bf16[128,2048]{1,0:T(8,128)(2,1)}, u32[]{:S(2)}, u32[]{:S(2)}) collective-permute-start(bf16[128,2048]{1,0:T(8,128)(2,1)} %get-tuple-element.114.refs_0_), channel_id=1, source_target_pairs={{0,3},{1,2},{2,1},{3,0},{4,7},{5,6},{6,5},{7,4},{8,11},{9,10},{10,... | collective-permute-start | bytes 1572872 | tf_op jit(solution)/shard_map/ppermute | solution.py:19
  262.9 41.2 %collective-permute-start.37 = (bf16[256,2048]{1,0:T(8,128)(2,1)}, bf16[256,2048]{1,0:T(8,128)(2,1)}, u32[]{:S(2)}, u32[]{:S(2)}) collective-permute-start(bf16[256,2048]{1,0:T(8,128)(2,1)} %add_parts.11.refs_11_), channel_id=1, source_target_pairs={{0,8},{4,12},{8,0},{12,4},{16,24},{20,28},{24,16},{28,20},{1,9},{5... | collective-permute-start | bytes 3145736 | tf_op jit(solution)/shard_map/ppermute | solution.py:19
  277.2 45.9 %collective-permute-start.41 = (bf16[256,2048]{1,0:T(8,128)(2,1)}, bf16[256,2048]{1,0:T(8,128)(2,1)}, u32[]{:S(2)}, u32[]{:S(2)}) collective-permute-start(bf16[256,2048]{1,0:T(8,128)(2,1)} %add_parts.12.refs_14_), channel_id=1, source_target_pairs={{0,8},{4,12},{8,0},{12,4},{16,24},{20,28},{24,16},{28,20},{1,9},{5... | collective-permute-start | bytes 3145736 | tf_op jit(solution)/shard_map/ppermute | solution.py:19
  300.6 38.6 %collective-permute-start.43 = (bf16[256,2048]{1,0:T(8,128)(2,1)}, bf16[256,2048]{1,0:T(8,128)(2,1)S(1)}, u32[]{:S(2)}, u32[]{:S(2)}) collective-permute-start(bf16[256,2048]{1,0:T(8,128)(2,1)} %add_parts.13.refs_10_), channel_id=1, source_target_pairs={{0,8},{4,12},{8,0},{12,4},{16,24},{20,28},{24,16},{28,20},{1,9},{5... | collective-permute-start | bytes 3145736 | tf_op jit(solution)/shard_map/ppermute | solution.py:19
  343.1 25.7 %collective-permute-start.48 = (bf16[512,512]{1,0:T(8,128)(2,1)}, bf16[512,512]{1,0:T(8,128)(2,1)S(1)}, u32[]{:S(2)}, u32[]{:S(2)}) collective-permute-start(bf16[512,512]{1,0:T(8,128)(2,1)} %add_parts.14.refs_2_), channel_id=1, source_target_pairs={{0,8},{4,12},{8,0},{12,4},{16,24},{20,28},{24,16},{28,20},{1,9},{5... | collective-permute-start | bytes 1572872 | tf_op jit(solution)/shard_map/ppermute | solution.py:19
  351.4 24.6 %collective-permute-start.51 = (bf16[512,512]{1,0:T(8,128)(2,1)}, bf16[512,512]{1,0:T(8,128)(2,1)S(1)}, u32[]{:S(2)}, u32[]{:S(2)}) collective-permute-start(bf16[512,512]{1,0:T(8,128)(2,1)} %add_parts.15.refs_2_), channel_id=1, source_target_pairs={{0,8},{4,12},{8,0},{12,4},{16,24},{20,28},{24,16},{28,20},{1,9},{5... | collective-permute-start | bytes 1572872 | tf_op jit(solution)/shard_map/ppermute | solution.py:19
  353.7 48.3 %collective-permute-start.53 = (bf16[512,512]{1,0:T(8,128)(2,1)}, bf16[512,512]{1,0:T(8,128)(2,1)S(1)}, u32[]{:S(2)}, u32[]{:S(2)}) collective-permute-start(bf16[512,512]{1,0:T(8,128)(2,1)} %add_parts.16.refs_2_), channel_id=1, source_target_pairs={{0,8},{4,12},{8,0},{12,4},{16,24},{20,28},{24,16},{28,20},{1,9},{5... | collective-permute-start | bytes 1572872 | tf_op jit(solution)/shard_map/ppermute | solution.py:19
  361.7 46.6 %collective-permute-start.55 = (bf16[512,512]{1,0:T(8,128)(2,1)}, bf16[512,512]{1,0:T(8,128)(2,1)S(1)}, u32[]{:S(2)}, u32[]{:S(2)}) collective-permute-start(bf16[512,512]{1,0:T(8,128)(2,1)} %add_parts.17.refs_1_), channel_id=1, source_target_pairs={{0,8},{4,12},{8,0},{12,4},{16,24},{20,28},{24,16},{28,20},{1,9},{5... | collective-permute-start | bytes 1572872 | tf_op jit(solution)/shard_map/ppermute | solution.py:19
  371.5 30.6 %collective-permute-start.50 = (bf16[256,512]{1,0:T(8,128)(2,1)}, bf16[256,512]{1,0:T(8,128)(2,1)S(1)}, u32[]{:S(2)}, u32[]{:S(2)}) collective-permute-start(bf16[256,512]{1,0:T(8,128)(2,1)} %add_parts.18.refs_3_), channel_id=1, source_target_pairs={{0,16},{4,20},{8,24},{12,28},{16,0},{20,4},{24,8},{28,12},{1,17},{... | collective-permute-start | bytes 786440 | tf_op jit(solution)/shard_map/ppermute | solution.py:19
  378.6 29.7 %collective-permute-start.52 = (bf16[256,512]{1,0:T(8,128)(2,1)}, bf16[256,512]{1,0:T(8,128)(2,1)S(1)}, u32[]{:S(2)}, u32[]{:S(2)}) collective-permute-start(bf16[256,512]{1,0:T(8,128)(2,1)} %add_parts.19.refs_3_), channel_id=1, source_target_pairs={{0,16},{4,20},{8,24},{12,28},{16,0},{20,4},{24,8},{28,12},{1,17},{... | collective-permute-start | bytes 786440 | tf_op jit(solution)/shard_map/ppermute | solution.py:19
  402.0 31.1 %collective-permute-start.58 = (f32[4,512]{1,0:T(4,128)S(1)}, f32[4,512]{1,0:T(4,128)S(1)}, u32[]{:S(2)}, u32[]{:S(2)}) collective-permute-start(f32[4,512]{1,0:T(4,128)S(1)} %add.101.refs_5_), channel_id=1, source_target_pairs={{0,16},{4,20},{8,24},{12,28},{16,0},{20,4},{24,8},{28,12},{1,17},{... | collective-permute-start | bytes 24584 | tf_op jit(solution)/shard_map/ppermute | solution.py:19
  (82 other events, 771.7 us)
